TPU v7x, 32 devices: a whole 2x2x4 slice. The times are simulated.
32 devices in a mesh: grp: 4 (over y, core), sp: 8 (over z, x).
Axes of the slice: x: 2, y: 2, z: 4, core: 2. Of those that a mesh axis runs over, the one named last changes fastest.
Arguments:
- flame_state: float32 [54, 16, 512], P(None, 'sp', 'grp'), may hold values from -1 to 2, as said below
- tangents: float32 [12, 54, 16, 512], P('grp', None, 'sp'), may hold values from -6 to 6
- direction_index: int32 [12], P('grp'), may hold values from 0 to 324
- reactant_table: int32 [325, 53], replicated, may hold values from 0 to 2, as said below
- product_table: int32 [325, 53], replicated, may hold values from 0 to 2, as said below
- natural_log_frequency: float32 [325], replicated, may hold values from -3 to -1
- arrhenius_energy: float32 [325], replicated, may hold values from 0.5 to 3
- diffusivity: float32 [54], replicated, may hold values from 0.03 to 0.25
- enthalpy: float32 [53], replicated, may hold values from -0.5 to 0.5
Outputs:
- new_state: float32 [54, 16, 512], P(None, 'sp', 'grp')
- new_tangents: float32 [12, 54, 16, 512], P('grp', None, 'sp')
Inputs may be any that keep to these rules, and one draw needn't show every extreme that they name: `flame_state`: rows 0 to 52 are log concentrations in [-1, 0.5]; the last row is temperature in [1, 2]. `reactant_table`: each reaction has one or two reactant units; a species may count twice. `product_table`: each reaction has one or two product units; a species may count twice.
All inputs are finite; a program needn't handle non-finite values.
Results may differ from a plain program's by a relative error of at most 0.0003.
Values sent between devices are 32-bit elements; how exact they have to be, the bound alone decides.
A program may use at most 128 MiB of HBM per device.

v0:
```python
import math

import jax
import jax.numpy as jnp
from jax import lax
from jax.sharding import PartitionSpec as P

GRID_POINTS_THREE = 32


time_step = 0.2
maximum_magnitude = lax.Precision.HIGHEST


def padded_2(block, sides, width):
    for axis, dim in sides:
        count = lax.axis_size(axis)
        forward = [(i, i + 1) for i in range(count - 1)]
        forward.append((count - 1, 0))
        backward = [(target, source) for source, target in forward]
        low = lax.ppermute(
            lax.slice_in_dim(block, block.shape[dim] - width, None, axis=dim), axis, forward
        )
        high = lax.ppermute(lax.slice_in_dim(block, 0, width, axis=dim), axis, backward)
        block = jnp.concatenate([low, block, high], axis=dim)
    return block


def blockwise(kernel, arrays, block_cells):
    blocks = arrays[0].shape[-1] // block_cells

    def advance(block_id, results):
        pieces = [operand_array for operand_array in arrays]
        stored_numbers = kernel(*pieces)
        return tuple((value for value in stored_numbers))

    return lax.fori_loop(
        0, blocks, advance, tuple((jnp.zeros_like(operand_array) for operand_array in arrays))
    )


def progress(stored_numbers, tables):
    consumed_multipliers, nu_net, natural_log_frequency, arrhenius_energy, enthalpy = tables
    exponent_numbers = stored_numbers[:-1]
    mixture_heat_level = stored_numbers[-1]
    exponent_speed = (
        natural_log_frequency[:, None]
        - arrhenius_energy[:, None] / mixture_heat_level[None, :]
        + jnp.dot(consumed_multipliers, exponent_numbers, precision=maximum_magnitude)
    )
    reaction_rates = jnp.exp(exponent_speed)
    production = jnp.dot(nu_net.T, reaction_rates, precision=maximum_magnitude)
    return (reaction_rates, production)


def joint_chem(stored_numbers, derivative_direction, selection_filter, tables):
    consumed_multipliers, nu_net, natural_log_frequency, arrhenius_energy, enthalpy = tables
    reaction_rates, production = progress(stored_numbers, tables)
    mixture_heat_level = stored_numbers[-1]
    inverse = jnp.exp(-stored_numbers[:-1])
    tangent_logs = derivative_direction[:, :-1]
    derivative_thermal_field = derivative_direction[:, -1]
    exponent_shift = (
        selection_filter[:, :, None]
        + arrhenius_energy[None, :, None]
        / (mixture_heat_level * mixture_heat_level)[None, None, :]
        * derivative_thermal_field[:, None, :]
    )
    exponent_shift = exponent_shift + jnp.einsum(
        "rs,dsb->drb", consumed_multipliers, tangent_logs, precision=maximum_magnitude
    )
    production_change = jnp.einsum(
        "rs,drb->dsb", nu_net, reaction_rates[None] * exponent_shift, precision=maximum_magnitude
    )
    heat_change = -jnp.einsum("s,dsb->db", enthalpy, production_change, precision=maximum_magnitude)
    heat_term = -jnp.dot(enthalpy, production, precision=maximum_magnitude)
    nominal = jnp.concatenate([production * inverse, heat_term[None, :]], 0)
    tangent_change = jnp.concatenate(
        [
            (production_change - production[None] * tangent_logs) * inverse[None],
            heat_change[:, None, :],
        ],
        1,
    )
    return (nominal, tangent_change)


def trimmed(operand_array, dimension, leading_cut, trailing_cut):
    return lax.slice_in_dim(
        operand_array, leading_cut, operand_array.shape[dimension] - trailing_cut, axis=dimension
    )


def laplace_padded(padded, dimension):
    centre = trimmed(padded, dimension, 1, 1)
    first_sides = trimmed(padded, dimension, 2, 0) + trimmed(padded, dimension, 0, 2)
    second_sides = jnp.roll(centre, 1, dimension + 1) + jnp.roll(centre, -1, dimension + 1)
    third_sides = jnp.roll(centre, 1, dimension + 2) + jnp.roll(centre, -1, dimension + 2)
    return first_sides + second_sides + third_sides - 6.0 * centre


def laplace_cells(padded, dimension):
    shaped = padded.reshape(
        padded.shape[:-1] + (padded.shape[-1] // GRID_POINTS_THREE, GRID_POINTS_THREE)
    )
    result = laplace_padded(shaped, dimension)
    return result.reshape(result.shape[:-2] + (result.shape[-2] * GRID_POINTS_THREE,))


def shards(
    flame_state,
    tangents,
    direction_index,
    reactant_table,
    product_table,
    natural_log_frequency,
    arrhenius_energy,
    diffusivity,
    enthalpy,
):
    fields = flame_state.shape[0]
    reactions = reactant_table.shape[0]
    tables = (
        reactant_table.astype(jnp.float32),
        (product_table - reactant_table).astype(jnp.float32),
        natural_log_frequency,
        arrhenius_energy,
        enthalpy,
    )
    selection_filter = (
        direction_index[:, None] == jnp.arange(reactions, dtype=jnp.int32)[None, :]
    ).astype(jnp.float32)
    spread = diffusivity[:, None, None]
    tangent_spread = diffusivity[None, :, None, None]

    def joint_kernel(portion, tangent_portion):
        return joint_chem(portion, tangent_portion, selection_filter, tables)

    def block_size(flattened, plane_cells):
        return plane_cells * math.gcd(8, flattened.shape[1] // plane_cells)

    def tile_halo(stored_numbers):
        return padded_2(stored_numbers, (("sp", 1),), 1)

    def tangent_halo(stored_numbers):
        return padded_2(stored_numbers, (("sp", 2),), 1)

    def tangent_rate(stored_numbers, padded):
        interior = trimmed(padded, 2, 1, 1)
        flattened = stored_numbers.reshape(fields, -1)
        combined = blockwise(
            joint_kernel,
            (flattened, interior.reshape(interior.shape[0], fields, -1)),
            block_size(flattened, stored_numbers.shape[-1]),
        )
        chemical = combined[1].reshape(interior.shape)
        return (
            combined[0].reshape(stored_numbers.shape),
            chemical + tangent_spread * laplace_cells(padded, 2),
        )

    gathered_start = lax.all_gather(flame_state, "grp", axis=2, tiled=True)
    tile_pad = tile_halo(gathered_start)
    start_chem, start_change = tangent_rate(gathered_start, tangent_halo(tangents))
    middle_tangent_pad = tangent_halo(tangents + time_step * start_change)
    tile_rate = start_chem + spread * laplace_cells(tile_pad, 1)
    middle_tile = gathered_start + time_step * tile_rate
    middle_tile_pad = tile_halo(middle_tile)
    middle_chem, middle_change = tangent_rate(middle_tile, middle_tangent_pad)
    middle_tile_rate = middle_chem + spread * laplace_cells(middle_tile_pad, 1)
    whole_new = gathered_start + 0.5 * time_step * (tile_rate + middle_tile_rate)
    row_cells = flame_state.shape[2]
    new_state = lax.dynamic_slice_in_dim(whole_new, lax.axis_index("grp") * row_cells, row_cells, 2)
    new_tangents = tangents + 0.5 * time_step * (start_change + middle_change)
    return (new_state, new_tangents)


def solution(mesh):
    in_specs = (
        P(None, "sp", "grp"),
        P("grp", None, "sp", None),
        P("grp"),
        P(),
        P(),
        P(),
        P(),
        P(),
        P(),
    )
    out_specs = (P(None, "sp", "grp"), P("grp", None, "sp", None))
    return jax.shard_map(shards, mesh=mesh, in_specs=in_specs, out_specs=out_specs, check_vma=False)
```

profile of v0, /device:TPU:0, one launch (start us, length us, event | category | flops | bytes accessed | tf_op | source)
XLA Modules:
  0.0 122.4 jit_solution(212196987079707872)
XLA Ops:
  0.7 1.0 copy.72
  1.6 8.7 %all_gather.3 = f32[54,2,512]{0,2,1:T(8,128)S(1)} all-gather(f32[54,2,128]{0,2,1:T(8,128)S(1)} %copy.72), channel_id=1, replica_groups=mesh['grp'=4,'sp'=8] {'grp'}, dimensions={2}, use_global_device_ids=true | all-gather | bytes 276480 | tf_op jit(solution)/shard_map/all_gather | solution.py:162
  10.3 0.8 fusion.94
  11.1 4.5 %collective-permute-start.1 = (f32[54,1,512]{0,2,1:T(8,128)}, f32[54,1,512]{0,2,1:T(8,128)}, u32[]{:S(2)}, u32[]{:S(2)}) collective-permute-start(f32[54,1,512]{0,2,1:T(8,128)} %get-tuple-element.113), channel_id=1, source_target_pairs={{1,0},{2,1},{3,2},{4,3},{5,4},{6,5},{7,6},{0,7},{9,8},{10,9},{11,1... | collective-permute-start | bytes 331784 | tf_op jit(solution)/shard_map/ppermute | solution.py:24
  15.7 1.4 %fusion.92 = (f32[3,54,1,512]{3,2,1,0:T(1,128)}, f32[3,54,1,512]{3,2,1,0:T(1,128)}) fusion(f32[3,54,2,512]{3,2,1,0:T(2,128)S(1)} %copy-done.9), kind=kLoop, calls=%fused_computation.136 | loop fusion | bytes 1327104 | tf_op jit(solution)/shard_map/slice | solution.py:22
  17.0 4.7 %collective-permute-start.5 = (f32[3,54,1,512]{3,2,1,0:T(1,128)}, f32[3,54,1,512]{3,2,1,0:T(1,128)}, u32[]{:S(2)}, u32[]{:S(2)}) collective-permute-start(f32[3,54,1,512]{3,2,1,0:T(1,128)} %get-tuple-element.109), channel_id=1, source_target_pairs={{1,0},{2,1},{3,2},{4,3},{5,4},{6,5},{7,6},{0,7},{9,8},{10,9},{11,1... | collective-permute-start | bytes 995336 | tf_op jit(solution)/shard_map/ppermute | solution.py:24
  22.1 1.6 %copy.88 = f32[3,54,2,512]{1,3,2,0:T(8,128)} copy(f32[3,54,2,512]{3,2,1,0:T(2,128)S(1)} %copy-done.9) | data formatting | bytes 1327104 | tf_op args[1]
  23.8 0.6 reshape.174
  24.7 5.0 %fusion.36 = f32[3,1024,325]{1,2,0:T(8,128)} fusion(f32[3,54,1024]{2,1,0:T(8,128)S(1)} %reshape.174, s32[325,53]{0,1:T(8,128)S(1)} %copy-done.19), kind=kOutput, calls=%fused_computation.57 | convolution fusion | flops 634999616 | bytes 4726052 | tf_op jit(solution)/shard_map/while/body/eval_jaxpr/rs,dsb->drb/dot_general | solution.py:69
  29.7 1.5 %fusion.29 = f32[325,1024]{1,0:T(8,128)S(1)} fusion(f32[53,1024]{0,1:T(8,128)S(1)} %bitcast.130, f32[1024]{0:T(1024)S(1)} %bitcast.141, f32[325]{0:T(512)S(1)} %copy-done.26, f32[325]{0:T(512)S(1)} %copy-done.29, s32[325,53]{0,1:T(8,128)S(1)} %copy-done.19), kind=kOutput, calls=%fused_computation.45 | convolution fusion | flops 212676416 | bytes 1623884 | tf_op jit(solution)/shard_map/while/body/eval_jaxpr/dot_general | solution.py:49
  31.2 1.1 copy-done.12
  32.3 1.6 %negate_exponential_fusion.1 = (f32[53,1024]{1,0:T(8,128)}, f32[53,1024]{1,0:T(8,128)S(1)}, f32[53,1024]{1,0:T(8,128)S(1)}) fusion(f32[53,1024]{1,0:T(8,128)S(1)} %copy.93, f32[325,1024]{1,0:T(8,128)S(1)} %fusion.29, s32[325,53]{0,1:T(8,128)S(1)} %sub.45), kind=kOutput, calls=%fused_computation.79 | convolution fusion | flops 211786560 | bytes 2268452 | tf_op jit(solution)/shard_map/while/body/eval_jaxpr/dot_general | solution.py:52
  34.3 0.7 fusion.62
  35.3 1.1 pad_maximum_fusion.2
  37.4 0.9 multiply_add_fusion.1
  38.7 0.9 fusion.93
  39.7 2.5 %fusion.28 = f32[325,1024]{1,0:T(8,128)} fusion(f32[53,1024]{0,1:T(8,128)S(1)} %bitcast.134, f32[1024]{0:T(1024)S(1)} %bitcast.142, f32[325]{0:T(512)S(1)} %copy-done.26, f32[325]{0:T(512)S(1)} %copy-done.29, s32[325,53]{0,1:T(8,128)S(1)} %copy-done.19), kind=kOutput, calls=%fused_computation.43 | convolution fusion | flops 212676416 | bytes 1623884 | tf_op jit(solution)/shard_map/while/body/eval_jaxpr/dot_general | solution.py:49
  42.3 2.9 %negate_exponential_fusion = (f32[53,1024]{1,0:T(8,128)}, f32[53,1024]{1,0:T(8,128)S(1)}, f32[53,1024]{1,0:T(8,128)S(1)}) fusion(f32[53,1024]{1,0:T(8,128)S(1)} %copy.94, f32[325,1024]{1,0:T(8,128)} %fusion.28, s32[325,53]{0,1:T(8,128)S(1)} %sub.45), kind=kOutput, calls=%fused_computation.78 | convolution fusion | flops 211786560 | bytes 2268452 | tf_op jit(solution)/shard_map/while/body/eval_jaxpr/dot_general | solution.py:52
  45.4 0.9 concatenate.112
  46.3 4.7 %collective-permute-start.3 = (f32[54,1,512]{0,2,1:T(8,128)}, f32[54,1,512]{0,2,1:T(8,128)}, u32[]{:S(2)}, u32[]{:S(2)}) collective-permute-start(f32[54,1,512]{0,2,1:T(8,128)} %get-tuple-element.111), channel_id=1, source_target_pairs={{1,0},{2,1},{3,2},{4,3},{5,4},{6,5},{7,6},{0,7},{9,8},{10,9},{11,1... | collective-permute-start | bytes 331784 | tf_op jit(solution)/shard_map/ppermute | solution.py:24
  51.1 1.4 %broadcast_divide_fusion = (f32[325,1024]{1,0:T(8,128)}, f32[325,1024]{1,0:T(8,128)S(1)}) fusion(f32[1024]{0:T(1024)S(1)} %mul.234, f32[325]{0:T(512)S(1)} %copy-done.27, f32[1024]{0:T(1024)S(1)} %mul.220), kind=kLoop, calls=%fused_computation.55 | loop fusion | flops 665600 | bytes 2671892 | tf_op jit(solution)/shard_map/while/body/eval_jaxpr/div | solution.py:65
  52.5 6.1 %subtract_multiply_fusion.1 = (f32[3,53,1024]{2,1,0:T(8,128)S(1)}, f32[3,53,1024]{2,1,0:T(8,128)S(1)}) fusion(f32[3,54,1024]{2,1,0:T(8,128)S(1)} %reshape.174, f32[53,1024]{1,0:T(8,128)S(1)} %copy-done.17, f32[53,1024]{1,0:T(8,128)S(1)} %copy-done.15, s32[325,53]{0,1:T(8,128)S(1)} %sub.45, f32[3,1024,325]{1,2,0:T(8,128)} %fusion.36, ...), kind=kOutput, calls=%fused_computation.54 | convolution fusion | flops 639481664 | bytes 9129056 | tf_op jit(solution)/shard_map/while/body/eval_jaxpr/rs,drb->dsb/dot_general | solution.py:72
  59.3 0.8 copy.103
  60.0 2.6 %concatenate.136 = f32[3,1,2,512]{1,3,2,0:T(8,128)} reshape(f32[3,1024]{1,0:T(4,128)S(1)} %bitcast_negate_fusion.1) | data formatting | bytes 24576 | tf_op jit(solution)/shard_map/while/body/eval_jaxpr/concatenate | solution.py:78
  62.7 1.8 %copy.95 = f32[3,53,1024]{1,2,0:T(8,128)} copy(f32[3,53,1024]{2,1,0:T(8,128)S(1)} %get-tuple-element.122) | data formatting | bytes 1302528 | tf_op jit(solution)/shard_map/while/body/eval_jaxpr/concatenate | solution.py:78
  64.4 1.1 pad_maximum_fusion.3
  66.7 1.0 dynamic-slice_add_fusion
  67.7 0.7 copy.89
  68.4 3.1 %pad_maximum_fusion.1 = f32[3,54,4,512]{3,2,1,0:T(4,128)} fusion(f32[3,54,1,512]{3,2,1,0:T(1,128)} %collective-permute-done.5, f32[3,54,2,512]{3,2,1,0:T(2,128)S(1)} %copy-done.9, f32[3,54,1,512]{3,2,1,0:T(1,128)} %collective-permute-done.4), kind=kLoop, calls=%fused_computation.48 | loop fusion | flops 663552 | bytes 2654208 | tf_op jit(solution)/shard_map/concatenate | solution.py:25
  71.5 2.1 %copy.79 = f32[3,54,4,512]{1,3,2,0:T(8,128)S(1)} copy(f32[3,54,4,512]{3,2,1,0:T(4,128)} %pad_maximum_fusion.1) | data formatting | bytes 2654208 | tf_op jit(solution)/shard_map/concatenate | solution.py:25
  74.7 1.3 %fusion.21 = f32[3,54,2,16,32]{1,4,3,2,0:T(8,128)S(1)} fusion(f32[3,54,4,16,32]{1,4,3,2,0:T(8,128)S(1)} %bitcast.115, f32[3,54,2,15,32]{1,4,3,2,0:T(8,128)S(1)} %get-tuple-element.76, f32[3,54,2,1,32]{1,4,3,2,0:T(8,128)S(1)} %get-tuple-element.89, f32[3,54,2,1,32]{1,4,3,2,0:T(8,128)S(1)} %get-tuple-element.88, ...), kind=kLoop, calls=%fused_computation.25 | loop fusion | flops 1824768 | bytes 5308416 | tf_op jit(solution)/shard_map/sub | solution.py:99
  76.6 0.6 copy-done.7
  77.7 5.3 %fusion.49 = f32[3,1024,325]{1,2,0:T(8,128)} fusion(s32[325,53]{0,1:T(8,128)S(1)} %copy-done.19, f32[3,54,1024]{1,2,0:T(8,128)S(1)} %bitcast.116), kind=kOutput, calls=%fused_computation.89 | convolution fusion | flops 634999616 | bytes 4726052 | tf_op jit(solution)/shard_map/while/body/eval_jaxpr/rs,dsb->drb/dot_general | solution.py:69
  83.4 1.3 %fusion.83 = (f32[3,54,1,512]{1,3,2,0:T(8,128)}, f32[3,54,1,512]{1,3,2,0:T(8,128)}) fusion(f32[3,54,2,512]{1,3,2,0:T(8,128)S(1)} %multiply_add_fusion), kind=kLoop, calls=%fused_computation.127 | loop fusion | bytes 1327104 | tf_op jit(solution)/shard_map/slice | solution.py:22
  84.7 1.4 %copy.101 = f32[3,53,1024]{2,1,0:T(8,128)} copy(f32[3,53,1024]{1,2,0:T(8,128)S(1)} %bitcast.118) | data formatting | bytes 1302528
  86.1 0.6 copy.99
  86.7 2.1 %copy.85 = f32[3,54,1,512]{3,2,1,0:T(1,128)} copy(f32[3,54,1,512]{1,3,2,0:T(8,128)} %get-tuple-element.91) | data formatting | bytes 663552 | tf_op jit(solution)/shard_map/slice | solution.py:24
  88.8 4.7 %collective-permute-start.7 = (f32[3,54,1,512]{3,2,1,0:T(1,128)}, f32[3,54,1,512]{3,2,1,0:T(1,128)}, u32[]{:S(2)}, u32[]{:S(2)}) collective-permute-start(f32[3,54,1,512]{3,2,1,0:T(1,128)} %copy.85), channel_id=1, source_target_pairs={{1,0},{2,1},{3,2},{4,3},{5,4},{6,5},{7,6},{0,7},{9,8},{10,9},{11,1... | collective-permute-start | bytes 995336 | tf_op jit(solution)/shard_map/ppermute | solution.py:24
  93.5 2.0 %copy.84 = f32[3,54,1,512]{3,2,1,0:T(1,128)} copy(f32[3,54,1,512]{1,3,2,0:T(8,128)} %get-tuple-element.90) | data formatting | bytes 663552 | tf_op jit(solution)/shard_map/slice | solution.py:22
  95.5 7.6 %subtract_multiply_fusion = (f32[3,53,1024]{2,1,0:T(8,128)}, f32[3,53,1024]{2,1,0:T(8,128)S(1)}) fusion(f32[3,53,1024]{2,1,0:T(8,128)} %copy.101, f32[53,1024]{1,0:T(8,128)S(1)} %copy-done.16, f32[53,1024]{1,0:T(8,128)S(1)} %get-tuple-element.121, s32[325,53]{0,1:T(8,128)S(1)} %sub.45, f32[3,1024,325]{1,2,0:T(8,128)} %fusion.49, ...), kind=kOutput, calls=%fused_computation.53 | convolution fusion | flops 639481664 | bytes 9129056 | tf_op jit(solution)/shard_map/while/body/eval_jaxpr/rs,drb->dsb/dot_general | solution.py:72
  103.6 1.5 %concatenate.137 = f32[3,1,2,512]{1,3,2,0:T(8,128)S(1)} reshape(f32[3,1024]{1,0:T(4,128)S(1)} %bitcast_negate_fusion) | data formatting | bytes 24576 | tf_op jit(solution)/shard_map/while/body/eval_jaxpr/concatenate | solution.py:78
  105.1 2.8 %copy.97 = f32[3,53,1024]{1,2,0:T(8,128)} copy(f32[3,53,1024]{2,1,0:T(8,128)} %get-tuple-element.124) | data formatting | bytes 1302528 | tf_op jit(solution)/shard_map/while/body/eval_jaxpr/concatenate | solution.py:78
  107.9 2.0 %copy.87 = f32[3,54,1,512]{1,3,2,0:T(8,128)} copy(f32[3,54,1,512]{3,2,1,0:T(1,128)} %collective-permute-done.7) | data formatting | bytes 663552 | tf_op jit(solution)/shard_map/ppermute | solution.py:24
  109.9 2.0 %copy.86 = f32[3,54,1,512]{1,3,2,0:T(8,128)} copy(f32[3,54,1,512]{3,2,1,0:T(1,128)} %collective-permute-done.6) | data formatting | bytes 663552 | tf_op jit(solution)/shard_map/ppermute | solution.py:21
  111.9 1.8 %pad_maximum_fusion = f32[3,54,4,512]{1,3,2,0:T(8,128)S(1)} fusion(f32[3,54,1,512]{1,3,2,0:T(8,128)} %copy.87, f32[3,54,2,512]{1,3,2,0:T(8,128)S(1)} %multiply_add_fusion, f32[3,54,1,512]{1,3,2,0:T(8,128)} %copy.86), kind=kLoop, calls=%fused_computation.10 | loop fusion | flops 663552 | bytes 2654208 | tf_op jit(solution)/shard_map/concatenate | solution.py:25
  114.7 1.3 %fusion.18 = f32[3,54,2,16,32]{1,4,3,2,0:T(8,128)S(1)} fusion(f32[3,54,4,16,32]{1,4,3,2,0:T(8,128)S(1)} %bitcast.110, f32[3,54,2,15,32]{1,4,3,2,0:T(8,128)S(1)} %get-tuple-element.68, f32[3,54,2,1,32]{1,4,3,2,0:T(8,128)S(1)} %get-tuple-element.70, f32[3,54,2,1,32]{1,4,3,2,0:T(8,128)S(1)} %get-tuple-element.69, ...), kind=kLoop, calls=%fused_computation.20 | loop fusion | flops 1824768 | bytes 5308416 | tf_op jit(solution)/shard_map/sub | solution.py:99
  117.9 2.1 %fusion.26 = f32[3,54,2,512]{1,3,2,0:T(8,128)} fusion(f32[3,54,2,512]{1,3,2,0:T(8,128)S(1)} %copy-done.4, f32[3,1,2,512]{1,3,2,0:T(8,128)S(1)} %concatenate.137, f32[3,53,2,512]{1,3,2,0:T(8,128)S(1)} %bitcast.135, f32[3,54,2,16,32]{1,4,3,2,0:T(8,128)S(1)} %fusion.18, f32[54]{0:T(128)S(1)} %copy-done.25, f32[3,54,2,16,32]{1,4,3,2,0:T(8,128)S(1)} %copy-done.2, ...), kind=kLoop, calls=%fused_computation.35 | loop fusion | flops 1492992 | bytes 3981528 | tf_op jit(solution)/shard_map/add | solution.py:174
  120.0 2.4 %copy.90 = f32[3,54,2,512]{3,2,1,0:T(2,128)} copy(f32[3,54,2,512]{1,3,2,0:T(8,128)} %fusion.26) | data formatting | bytes 1327104
  (116 shorter events, 10.9 us)
Async XLA Ops:
  0.6 33.2 %copy-start = (f32[53]{0:T(128)S(1)}, f32[53]{0:T(128)}, u32[]{:S(2)}) copy-start(f32[53]{0:T(128)} %param.17) | copy-start | bytes 640
  0.6 15.0 %copy-start.9 = (f32[3,54,2,512]{3,2,1,0:T(2,128)S(1)}, f32[3,54,2,512]{3,2,1,0:T(2,128)}, u32[]{:S(2)}) copy-start(f32[3,54,2,512]{3,2,1,0:T(2,128)} %param.10) | copy-start | bytes 1990660
  11.1 24.2 %collective-permute-start.1 = (f32[54,1,512]{0,2,1:T(8,128)}, f32[54,1,512]{0,2,1:T(8,128)}, u32[]{:S(2)}, u32[]{:S(2)}) collective-permute-start(f32[54,1,512]{0,2,1:T(8,128)} %get-tuple-element.113), channel_id=1, source_target_pairs={{1,0},{2,1},{3,2},{4,3},{5,4},{6,5},{7,6},{0,7},{9,8},{10,9},{11,1... | collective-permute-start | bytes 331784 | tf_op jit(solution)/shard_map/ppermute | solution.py:24
  15.7 19.6 %collective-permute-start = (f32[54,1,512]{0,2,1:T(8,128)}, f32[54,1,512]{0,2,1:T(8,128)}, u32[]{:S(2)}, u32[]{:S(2)}) collective-permute-start(f32[54,1,512]{0,2,1:T(8,128)} %get-tuple-element.112), channel_id=1, source_target_pairs={{0,1},{1,2},{2,3},{3,4},{4,5},{5,6},{6,7},{7,0},{8,9},{9,10},{10,1... | collective-permute-start | bytes 331784 | tf_op jit(solution)/shard_map/ppermute | solution.py:21
  17.0 51.4 %collective-permute-start.5 = (f32[3,54,1,512]{3,2,1,0:T(1,128)}, f32[3,54,1,512]{3,2,1,0:T(1,128)}, u32[]{:S(2)}, u32[]{:S(2)}) collective-permute-start(f32[3,54,1,512]{3,2,1,0:T(1,128)} %get-tuple-element.109), channel_id=1, source_target_pairs={{1,0},{2,1},{3,2},{4,3},{5,4},{6,5},{7,6},{0,7},{9,8},{10,9},{11,1... | collective-permute-start | bytes 995336 | tf_op jit(solution)/shard_map/ppermute | solution.py:24
  21.8 46.6 %collective-permute-start.4 = (f32[3,54,1,512]{3,2,1,0:T(1,128)}, f32[3,54,1,512]{3,2,1,0:T(1,128)}, u32[]{:S(2)}, u32[]{:S(2)}) collective-permute-start(f32[3,54,1,512]{3,2,1,0:T(1,128)} %get-tuple-element.108), channel_id=1, source_target_pairs={{0,1},{1,2},{2,3},{3,4},{4,5},{5,6},{6,7},{7,0},{8,9},{9,10},{10,1... | collective-permute-start | bytes 995336 | tf_op jit(solution)/shard_map/ppermute | solution.py:21
  23.8 0.9 copy-start.19
  24.7 5.0 %copy-start.21 = (s32[325,53]{0,1:T(8,128)S(1)}, s32[325,53]{0,1:T(8,128)}, u32[]{:S(2)}) copy-start(s32[325,53]{0,1:T(8,128)} %param.13) | copy-start | bytes 206704
  24.7 5.0 %copy-start.26 = (f32[325]{0:T(512)S(1)}, f32[325]{0:T(512)}, u32[]{:S(2)}) copy-start(f32[325]{0:T(512)} %param.15) | copy-start | bytes 3904
  24.7 5.0 %copy-start.29 = (f32[325]{0:T(512)S(1)}, f32[325]{0:T(512)}, u32[]{:S(2)}) copy-start(f32[325]{0:T(512)} %param.14) | copy-start | bytes 3904
  31.2 1.1 copy-start.12
  32.3 2.0 %copy-start.28 = (s32[3]{0:T(128)S(1)}, s32[3]{0:T(128)}, u32[]{:S(2)}) copy-start(s32[3]{0:T(128)} %param.11) | copy-start | bytes 40
  33.8 2.6 %copy-start.14 = (f32[53,1024]{1,0:T(8,128)}, f32[53,1024]{1,0:T(8,128)S(1)}, u32[]{:S(2)}) copy-start(f32[53,1024]{1,0:T(8,128)S(1)} %get-tuple-element.120) | copy-start | bytes 651268
  36.7 0.7 copy-start.24
  42.3 8.8 %copy-start.27 = (f32[325]{0:T(512)S(1)}, f32[325]{0:T(512)}, u32[]{:S(2)}) copy-start(f32[325]{0:T(512)} %param.15) | copy-start | bytes 3904
  45.4 7.0 %copy-start.22 = (f32[3,325]{1,0:T(4,128)S(1)}, f32[3,325]{1,0:T(4,128)}, u32[]{:S(2)}) copy-start(f32[3,325]{1,0:T(4,128)} %fusion.62) | copy-start | bytes 11704
  46.3 6.1 %copy-start.13 = (f32[325,1024]{1,0:T(8,128)S(1)}, f32[325,1024]{1,0:T(8,128)}, u32[]{:S(2)}) copy-start(f32[325,1024]{1,0:T(8,128)} %copy-done.12) | copy-start | bytes 3993604
  46.3 6.1 %copy-start.15 = (f32[53,1024]{1,0:T(8,128)S(1)}, f32[53,1024]{1,0:T(8,128)}, u32[]{:S(2)}) copy-start(f32[53,1024]{1,0:T(8,128)} %copy-done.14) | copy-start | bytes 651268
  46.3 6.1 %copy-start.17 = (f32[53,1024]{1,0:T(8,128)S(1)}, f32[53,1024]{1,0:T(8,128)}, u32[]{:S(2)}) copy-start(f32[53,1024]{1,0:T(8,128)} %get-tuple-element.116) | copy-start | bytes 651268
  46.3 18.1 %collective-permute-start.3 = (f32[54,1,512]{0,2,1:T(8,128)}, f32[54,1,512]{0,2,1:T(8,128)}, u32[]{:S(2)}, u32[]{:S(2)}) collective-permute-start(f32[54,1,512]{0,2,1:T(8,128)} %get-tuple-element.111), channel_id=1, source_target_pairs={{1,0},{2,1},{3,2},{4,3},{5,4},{6,5},{7,6},{0,7},{9,8},{10,9},{11,1... | collective-permute-start | bytes 331784 | tf_op jit(solution)/shard_map/ppermute | solution.py:24
  51.0 13.4 %collective-permute-start.2 = (f32[54,1,512]{0,2,1:T(8,128)}, f32[54,1,512]{0,2,1:T(8,128)}, u32[]{:S(2)}, u32[]{:S(2)}) collective-permute-start(f32[54,1,512]{0,2,1:T(8,128)} %get-tuple-element.110), channel_id=1, source_target_pairs={{0,1},{1,2},{2,3},{3,4},{4,5},{5,6},{6,7},{7,0},{8,9},{9,10},{10,1... | collective-permute-start | bytes 331784 | tf_op jit(solution)/shard_map/ppermute | solution.py:21
  52.4 6.7 %copy-start.18 = (f32[53,2,512]{2,1,0:T(2,128)S(1)}, f32[53,2,512]{2,1,0:T(2,128)}, u32[]{:S(2)}) copy-start(f32[53,2,512]{2,1,0:T(2,128)} %concatenate.112) | copy-start | bytes 651268
  65.8 0.9 copy-start.20
  65.8 0.9 copy-start.25
  74.7 1.4 %copy-start.3 = (f32[3,54,2,512]{1,3,2,0:T(8,128)S(1)}, f32[3,54,2,512]{1,3,2,0:T(8,128)}, u32[]{:S(2)}) copy-start(f32[3,54,2,512]{1,3,2,0:T(8,128)} %copy.88) | copy-start | bytes 1990660
  74.7 1.9 %copy-start.5 = (f32[3,1,2,512]{1,3,2,0:T(8,128)S(1)}, f32[3,1,2,512]{1,3,2,0:T(8,128)}, u32[]{:S(2)}) copy-start(f32[3,1,2,512]{1,3,2,0:T(8,128)} %concatenate.136) | copy-start | bytes 36868
  74.7 2.5 %copy-start.7 = (f32[3,53,1024]{1,2,0:T(8,128)S(1)}, f32[3,53,1024]{1,2,0:T(8,128)}, u32[]{:S(2)}) copy-start(f32[3,53,1024]{1,2,0:T(8,128)} %copy.95) | copy-start | bytes 1953796
  76.0 1.6 %copy-start.1 = (f32[3,54,2,16,32]{1,4,3,2,0:T(8,128)}, f32[3,54,2,16,32]{1,4,3,2,0:T(8,128)S(1)}, u32[]{:S(2)}) copy-start(f32[3,54,2,16,32]{1,4,3,2,0:T(8,128)S(1)} %fusion.21) | copy-start | bytes 1990660
  86.1 9.5 %copy-start.23 = (f32[3,325]{1,0:T(4,128)S(1)}, f32[3,325]{1,0:T(4,128)}, u32[]{:S(2)}) copy-start(f32[3,325]{1,0:T(4,128)} %fusion.62) | copy-start | bytes 11704
  86.7 8.9 %copy-start.11 = (f32[325,1024]{1,0:T(8,128)S(1)}, f32[325,1024]{1,0:T(8,128)}, u32[]{:S(2)}) copy-start(f32[325,1024]{1,0:T(8,128)} %get-tuple-element.118) | copy-start | bytes 3993604
  86.7 8.9 %copy-start.16 = (f32[53,1024]{1,0:T(8,128)S(1)}, f32[53,1024]{1,0:T(8,128)}, u32[]{:S(2)}) copy-start(f32[53,1024]{1,0:T(8,128)} %get-tuple-element.114) | copy-start | bytes 651268
  88.8 19.1 %collective-permute-start.7 = (f32[3,54,1,512]{3,2,1,0:T(1,128)}, f32[3,54,1,512]{3,2,1,0:T(1,128)}, u32[]{:S(2)}, u32[]{:S(2)}) collective-permute-start(f32[3,54,1,512]{3,2,1,0:T(1,128)} %copy.85), channel_id=1, source_target_pairs={{1,0},{2,1},{3,2},{4,3},{5,4},{6,5},{7,6},{0,7},{9,8},{10,9},{11,1... | collective-permute-start | bytes 995336 | tf_op jit(solution)/shard_map/ppermute | solution.py:24
  95.5 14.4 %collective-permute-start.6 = (f32[3,54,1,512]{3,2,1,0:T(1,128)}, f32[3,54,1,512]{3,2,1,0:T(1,128)}, u32[]{:S(2)}, u32[]{:S(2)}) collective-permute-start(f32[3,54,1,512]{3,2,1,0:T(1,128)} %copy.84), channel_id=1, source_target_pairs={{0,1},{1,2},{2,3},{3,4},{4,5},{5,6},{6,7},{7,0},{8,9},{9,10},{10,1... | collective-permute-start | bytes 995336 | tf_op jit(solution)/shard_map/ppermute | solution.py:21
  114.6 1.4 %copy-start.2 = (f32[3,54,2,16,32]{1,4,3,2,0:T(8,128)S(1)}, f32[3,54,2,16,32]{1,4,3,2,0:T(8,128)}, u32[]{:S(2)}) copy-start(f32[3,54,2,16,32]{1,4,3,2,0:T(8,128)} %copy-done.1) | copy-start | bytes 1990660
  114.6 1.9 %copy-start.4 = (f32[3,54,2,512]{1,3,2,0:T(8,128)S(1)}, f32[3,54,2,512]{1,3,2,0:T(8,128)}, u32[]{:S(2)}) copy-start(f32[3,54,2,512]{1,3,2,0:T(8,128)} %copy.88) | copy-start | bytes 1990660
  114.6 2.3 %copy-start.6 = (f32[3,1,2,512]{1,3,2,0:T(8,128)S(1)}, f32[3,1,2,512]{1,3,2,0:T(8,128)}, u32[]{:S(2)}) copy-start(f32[3,1,2,512]{1,3,2,0:T(8,128)} %concatenate.136) | copy-start | bytes 36868
  114.7 2.8 %copy-start.8 = (f32[3,53,1024]{1,2,0:T(8,128)S(1)}, f32[3,53,1024]{1,2,0:T(8,128)}, u32[]{:S(2)}) copy-start(f32[3,53,1024]{1,2,0:T(8,128)} %copy.95) | copy-start | bytes 1953796
  114.7 3.3 %copy-start.10 = (f32[3,53,1024]{1,2,0:T(8,128)S(1)}, f32[3,53,1024]{1,2,0:T(8,128)}, u32[]{:S(2)}) copy-start(f32[3,53,1024]{1,2,0:T(8,128)} %copy.97) | copy-start | bytes 1953796
where the time goes:
time: 123 us; the launch traced here: 122 us
  local copies, waits for them, and re-layouts  42.7 us (35%)
  matrix products  33.9 us (28%)
  starting transfers between devices  18.7 us (15%)
  other arithmetic  17.2 us (14%)
  blocking collectives  8.67 us (7%)
    ppermute x4, starting transfers between devices, padded_2(): lax.ppermute(lax.slice_in_dim(block, 0, width, axis=dim), axis, backward)  18.7 us
    dot_general x2, matrix products, joint_chem(): jnp.einsum('rs,drb->dsb', nu_net, reaction_rates[None] * exponent_shift,...  13.7 us
    unnamed x70, local copies, waits for them, and re-layouts  13.5 us
    dot_general x2, matrix products, joint_chem(): jnp.einsum('rs,dsb->drb', consumed_multipliers, tangent_logs, precision=m...  10.2 us
    all_gather x1, blocking collectives, shards(): gathered_start = lax.all_gather(flame_state, 'grp', axis=2, tiled=True)  8.67 us
    concatenate x4, local copies, waits for them, and re-layouts, joint_chem(): jnp.concatenate([(production_change - production[None] * tangent_logs) *...  8.61 us
    concatenate x4, other arithmetic, padded_2(): block = jnp.concatenate([low, block, high], axis=dim)  7.14 us
    slice x5, local copies, waits for them, and re-layouts, padded_2(): lax.slice_in_dim(block, block.shape[dim] - width, None, axis=dim)  6.33 us
  transfers between devices with their start and end apart: 8, of which 0 were waited for; matrix products, arithmetic and copies ran while one was open for 47% of the time, Pallas kernels for 0%

commit v1 on v0

v1 whole, which is shorter than its diff:
```python
import functools

import jax
import jax.numpy as jnp
from jax import lax
from jax.experimental import pallas as pl
from jax.experimental.pallas import tpu as pltpu
from jax.sharding import PartitionSpec as P

GRID_POINTS_THREE = 32
TIME_STEP = 0.2
ONE_LOW = 2.0**-10
MESH = pl.DeviceIdType.MESH
F32 = jnp.float32
BF16 = jnp.bfloat16


def in_plane(x, lane):
    cells = x.shape[1]
    width = GRID_POINTS_THREE
    before = jnp.where(
        lane == 0, pltpu.roll(x, cells - (width - 1), 1), pltpu.roll(x, 1, 1)
    )
    after = jnp.where(
        lane == width - 1, pltpu.roll(x, width - 1, 1), pltpu.roll(x, cells - 1, 1)
    )
    return before + after + (pltpu.roll(x, width, 1) + pltpu.roll(x, cells - width, 1))


def stacked(x, extra, species, row):
    base = species // 8 * 8
    tail = x[base:]
    tail = jnp.where(row == species + 1, 1.0 + ONE_LOW, jnp.where(row >= species, extra, tail))
    full = jnp.concatenate([x[:base], tail], 0)
    high = full.astype(BF16).astype(F32)
    return jnp.concatenate([high, full - high], 0).astype(BF16)


def with_heat(p, species, row, rest):
    base = species // 8 * 8
    tail = p[base:]
    heat = p[species : species + 1] + p[species + 1 : species + 2]
    tail = jnp.where(row < species, tail, jnp.where(row == species, heat, rest))
    return jnp.concatenate([p[:base], tail], 0), heat


def kernel(
    species, groups, ring,
    s_ref, t_ref, w_nominal, w_tangent, w_net, spread_ref,
    ns_ref, nt_ref,
    st, zs, mid, rates, prods, inverses, tt, mt, ns_full,
    st_send, st_recv, near_send, near_recv, far_send, far_recv, local_sem,
):
    directions = t_ref.shape[1]
    rows, cells = t_ref.shape[2], t_ref.shape[3]
    own_cells = s_ref.shape[2]
    g = lax.axis_index("grp")
    i = lax.axis_index("sp")
    odd = lax.rem(i, 2)
    partner = i + 1 - 2 * odd
    ahead = lax.rem(i + 2 - 4 * odd + ring, ring)
    behind = lax.rem(i - 2 + 4 * odd + ring, ring)
    near_side, far_side = 2 * (1 - odd), 2 * odd
    peers = [lax.rem(g + k, groups) for k in range(1, groups)]

    def remote(src, dst, send, recv, target):
        return pltpu.make_async_remote_copy(
            src_ref=src, dst_ref=dst, send_sem=send, recv_sem=recv,
            device_id=target, device_id_type=MESH,
        )

    own_t = pltpu.make_async_copy(t_ref, tt.at[pl.ds(2, 2)], local_sem.at[0])
    own_s = pltpu.make_async_copy(s_ref, st.at[1, g], local_sem.at[1])
    own_t.start()
    own_s.start()

    barrier = pltpu.get_barrier_semaphore()
    for target in [(g, partner), (g, ahead), (g, behind)] + [(p, i) for p in peers]:
        pl.semaphore_signal(barrier, inc=1, device_id=target, device_id_type=MESH)
    pl.semaphore_wait(barrier, 3 + len(peers))

    s_near = remote(s_ref, st.at[2 * odd, g], st_send.at[0], st_recv.at[2 * odd, g], (g, partner))
    s_near_in = remote(s_ref, st.at[near_side, g], st_send.at[0], st_recv.at[near_side, g], (g, partner))
    s_far = remote(st.at[near_side, g], st.at[far_side, g], st_send.at[1], st_recv.at[far_side, g], (g, ahead))

    def to_group(src, side, base):
        return [
            remote(src, st.at[side, g], st_send.at[base + k], st_recv.at[side, g], (p, i))
            for k, p in enumerate(peers)
        ]

    def near(d, p):
        return remote(
            t_ref.at[p, d], tt.at[4 * odd + p, d], near_send.at[d, p], near_recv.at[d, p], (g, partner)
        )

    def far(d, p):
        return remote(
            tt.at[4 * (1 - odd) + p, d], tt.at[4 * odd + p, d], far_send.at[d, p], far_recv.at[d, p], (g, ahead)
        )

    s_near.start()
    group_own = to_group(s_ref, 1, 2)
    for copy in group_own:
        copy.start()
    for d in range(directions):
        for p in range(2):
            near(d, p).start()

    s_near_in.wait_recv()
    s_far.start()
    group_near = to_group(st.at[near_side, g], near_side, 2 + len(peers))
    for copy in group_near:
        copy.start()
    s_far.wait_recv()
    group_far = to_group(st.at[far_side, g], far_side, 2 + 2 * len(peers))
    for copy in group_far:
        copy.start()

    def forward(d):
        for p in range(2):
            near(d, p).wait_recv()
            far(d, p).start()

    own_s.wait()
    for side in range(3):
        for p in peers:
            remote(
                st.at[side, p], st.at[side, p], st_send.at[0], st_recv.at[side, p], (p, i)
            ).wait_recv()
    for side in range(3):
        for q in range(groups):
            for p in range(2):
                zs[2 * side + p, :, q * own_cells : (q + 1) * own_cells] = st[side, q, p]
    own_t.wait()
    forward(0)

    row = lax.broadcasted_iota(jnp.int32, (rows - species // 8 * 8, cells), 0) + species // 8 * 8
    lane = lax.rem(
        lax.broadcasted_iota(jnp.int32, (rows, cells), 1), jnp.int32(GRID_POINTS_THREE)
    )
    spread = jnp.broadcast_to(spread_ref[:, :1], (rows, cells))

    def nominal(z, slot):
        level = 1.0 / z[species : species + 1]
        log_rate = jnp.dot(
            w_nominal[...], stacked(z, -level, species, row), preferred_element_type=F32
        )
        rate = jnp.exp(log_rate)
        rates[slot] = rate
        production = jnp.dot(w_net[...], rate.astype(BF16), preferred_element_type=F32)
        base = species // 8 * 8
        inverse = jnp.exp(-z)
        inverse = jnp.concatenate([inverse[:base], jnp.where(row < species, inverse[base:], 1.0)], 0)
        inverses[slot] = inverse
        plain = jnp.concatenate([production[:base], jnp.where(row < species, production[base:], 0.0)], 0)
        prods[slot] = plain
        total, _ = with_heat(production, species, row, 0.0)
        return total * inverse

    def tangent(u, level_squared, slot, d):
        change = jnp.dot(
            w_tangent[d],
            stacked(u, u[species : species + 1] * level_squared, species, row),
            preferred_element_type=F32,
        )
        moved = jnp.dot(
            w_net[...], (rates[slot] * change).astype(BF16), preferred_element_type=F32
        )
        moved, _ = with_heat(moved, species, row, 0.0)
        return (moved - prods[slot] * u) * inverses[slot]

    def squared(z):
        level = 1.0 / z[species : species + 1]
        return level * level

    def start_nominal(k, carry):
        z = zs[k + 1]
        lap = zs[k] + zs[k + 2] + in_plane(z, lane) - 6.0 * z
        rate = nominal(z, k) + spread * lap
        mid[k] = z + TIME_STEP * rate

        @pl.when((k == 1) | (k == 2))
        def _():
            ns_full[k - 1] = z + 0.5 * TIME_STEP * rate

        return carry

    lax.fori_loop(0, 4, start_nominal, 0)

    def middle_nominal(k, carry):
        z = mid[k + 1]
        lap = mid[k] + mid[k + 2] + in_plane(z, lane) - 6.0 * z
        ns_full[k] += 0.5 * TIME_STEP * (nominal(z, k + 4) + spread * lap)
        return carry

    lax.fori_loop(0, 2, middle_nominal, 0)
    for k in range(2):
        ns_ref[k] = ns_full[k, :, pl.ds(pl.multiple_of(g * own_cells, own_cells), own_cells)]

    fields = species + 1

    def direction(d, carry):
        @pl.when(d < directions - 1)
        def _():
            forward(d + 1)

        for p in range(2):
            far(d, p).wait_recv()

        def start_plane(k, carry):
            u = tt[k + 1, d]
            lap = tt[k, d] + tt[k + 2, d] + in_plane(u, lane) - 6.0 * u
            rate = tangent(u, squared(zs[k + 1]), k, d) + spread * lap
            mt[k] = u + TIME_STEP * rate

            @pl.when((k == 1) | (k == 2))
            def _():
                nt_ref[k - 1, d] = (u + 0.5 * TIME_STEP * rate)[:fields]

            return carry

        lax.fori_loop(0, 4, start_plane, 0)

        def middle_plane(k, carry):
            u = mt[k + 1]
            lap = mt[k] + mt[k + 2] + in_plane(u, lane) - 6.0 * u
            rate = tangent(u, squared(mid[k + 1]), k + 4, d) + spread * lap
            nt_ref[k, d] += (0.5 * TIME_STEP * rate)[:fields]
            return carry

        lax.fori_loop(0, 2, middle_plane, 0)
        return carry

    lax.fori_loop(0, directions, direction, 0)

    s_near.wait_send()
    s_far.wait_send()
    for copy in group_own + group_near + group_far:
        copy.wait_send()
    for d in range(directions):
        for p in range(2):
            near(d, p).wait_send()
            far(d, p).wait_send()


def split(x):
    high = lax.reduce_precision(x, 8, 7)
    return high, x - high


def shards(
    flame_state, tangents, direction_index, reactant_table, product_table,
    natural_log_frequency, arrhenius_energy, diffusivity, enthalpy,
):
    fields, planes, own_cells = flame_state.shape
    directions, cells = tangents.shape[0], tangents.shape[3]
    reactions, species = reactant_table.shape
    groups, ring = lax.axis_size("grp"), lax.axis_size("sp")
    assert planes == 2 and ring % 2 == 0
    rows = -(-(species + 3) // 8) * 8
    assert species % 8 <= 5
    depth = -(-reactions // 16) * 16

    state = jnp.pad(flame_state.transpose(1, 0, 2), ((0, 0), (0, rows - fields), (0, 0)))
    sens = jnp.pad(tangents.transpose(2, 0, 1, 3), ((0, 0), (0, 0), (0, rows - fields), (0, 0)))

    nu_in = reactant_table.astype(F32)
    nu_net = (product_table - reactant_table).astype(F32)
    e_high, e_low = split(arrhenius_energy)
    a_high, a_low = split(natural_log_frequency)
    zero = jnp.zeros((reactions, rows - species - 3), F32)

    def weights(one_high, one_low):
        def half(one):
            return [nu_in, e_high[:, None], one[:, None], e_low[:, None], zero]

        both = jnp.concatenate(half(one_high) + half(one_low), 1)
        return jnp.pad(both, ((0, depth - reactions), (0, 0))).astype(BF16)

    w_nominal = weights(a_high, a_low / ONE_LOW)
    chosen = (
        direction_index[:, None] == jnp.arange(reactions, dtype=jnp.int32)[None, :]
    ).astype(F32)
    w_tangent = jax.vmap(lambda one: weights(one, jnp.zeros_like(one)))(chosen)
    heat = -jnp.sum(nu_net * enthalpy[None, :], 1)
    h_high, h_low = split(heat)
    w_net = jnp.concatenate([nu_net, h_high[:, None], h_low[:, None]], 1).T
    w_net = jnp.pad(w_net, ((0, rows - species - 2), (0, depth - reactions))).astype(BF16)
    spread = jnp.broadcast_to(jnp.pad(diffusivity, (0, rows - fields))[:, None], (rows, 128))

    vmem = pl.BlockSpec(memory_space=pltpu.VMEM)
    anywhere = pl.BlockSpec(memory_space=pl.ANY)
    new_state, new_sens = pl.pallas_call(
        functools.partial(kernel, species, groups, ring),
        out_shape=(
            jax.ShapeDtypeStruct((2, rows, own_cells), F32),
            jax.ShapeDtypeStruct((2, directions, fields, cells), F32),
        ),
        in_specs=[anywhere, anywhere, vmem, vmem, vmem, vmem],
        out_specs=(vmem, vmem),
        scratch_shapes=[
            pltpu.VMEM((3, groups, 2, rows, own_cells), F32),
            pltpu.VMEM((6, rows, cells), F32),
            pltpu.VMEM((4, rows, cells), F32),
            pltpu.VMEM((6, depth, cells), F32),
            pltpu.VMEM((6, rows, cells), F32),
            pltpu.VMEM((6, rows, cells), F32),
            pltpu.VMEM((6, directions, rows, cells), F32),
            pltpu.VMEM((4, rows, cells), F32),
            pltpu.VMEM((2, rows, cells), F32),
            pltpu.SemaphoreType.DMA((2 + 3 * (groups - 1),)),
            pltpu.SemaphoreType.DMA((3, groups)),
            pltpu.SemaphoreType.DMA((directions, 2)),
            pltpu.SemaphoreType.DMA((directions, 2)),
            pltpu.SemaphoreType.DMA((directions, 2)),
            pltpu.SemaphoreType.DMA((directions, 2)),
            pltpu.SemaphoreType.DMA((2,)),
        ],
        compiler_params=pltpu.CompilerParams(
            collective_id=0, has_side_effects=True, vmem_limit_bytes=48 << 20
        ),
        name="step",
    )(state, sens, w_nominal, w_tangent, w_net, spread)
    return (
        new_state[:, :fields].transpose(1, 0, 2),
        new_sens.transpose(1, 2, 0, 3),
    )


def solution(mesh):
    in_specs = (
        P(None, "sp", "grp"), P("grp", None, "sp", None), P("grp"),
        P(), P(), P(), P(), P(), P(),
    )
    out_specs = (P(None, "sp", "grp"), P("grp", None, "sp", None))
    return jax.shard_map(shards, mesh=mesh, in_specs=in_specs, out_specs=out_specs, check_vma=False)
```

time: 123 us -> 47.1 us (0.38)
  Pallas kernels: 0 us -> 36.9 us
  local copies, waits for them, and re-layouts: 42.7 us -> 7.84 us
  matrix products: 33.9 us -> 0 us
  starting transfers between devices: 18.7 us -> 0 us
  other arithmetic: 17.2 us -> 1.25 us
  blocking collectives: 8.67 us -> 0 us
    pallas_call x0 -> x1, Pallas kernels: none -> 36.9 us  [shards(): pl.pallas_call(functools.partial(kernel, species, groups, ring), out_shap...]
    dot_general x12 -> x0, matrix products: 33.9 us -> none  [the longest x2 13.7 us: joint_chem(): jnp.einsum('rs,drb->dsb', nu_net, reaction_rates[None] * exponent_shift,...]
    ppermute x8 -> x0, starting transfers between devices: 18.7 us -> none  [the longest x4 18.7 us: padded_2(): lax.ppermute(lax.slice_in_dim(block, 0, width, axis=dim), axis, backward)]
    slice x28 -> x0, local copies, waits for them, and re-layouts: 12.5 us -> none  [the longest x5 6.33 us: padded_2(): lax.slice_in_dim(block, block.shape[dim] - width, None, axis=dim)]
    concatenate x10 -> x2, local copies, waits for them, and re-layouts: 12 us -> 1.25 us  [weights(): both = jnp.concatenate(half(one_high) + half(one_low), 1)]
    all_gather x1 -> x0, blocking collectives: 8.67 us -> none  [shards(): gathered_start = lax.all_gather(flame_state, 'grp', axis=2, tiled=True)]
    unnamed x70 -> x21, local copies, waits for them, and re-layouts: 13.5 us -> 5.01 us
    concatenate x6 -> x0, other arithmetic: 7.34 us -> none  [the longest x4 7.14 us: padded_2(): block = jnp.concatenate([low, block, high], axis=dim)]
  transfers between devices with their start and end apart: 8 -> 0, of which waited for: 0 -> 0; matrix products, arithmetic and copies ran while one was open for 47% -> 0% of each run, Pallas kernels for 0% -> 0%
where the time goes in v1:
time: 47.1 us; the launch traced here: 46.8 us
  Pallas kernels  36.9 us (78%)
  local copies, waits for them, and re-layouts  7.84 us (17%)
  other arithmetic  1.25 us (3%)
  between operations  0.84 us (2%)
    pallas_call x1, Pallas kernels, shards(): pl.pallas_call(functools.partial(kernel, species, groups, ring), out_shap...  36.9 us
    unnamed x21, local copies, waits for them, and re-layouts  5.01 us
    concatenate x2, local copies, waits for them, and re-layouts, weights(): both = jnp.concatenate(half(one_high) + half(one_low), 1)  1.25 us
    reduce_sum x1, other arithmetic, shards(): heat = -jnp.sum(nu_net * enthalpy[None, :], 1)  1.06 us

profile of v1, /device:TPU:0, one launch (start us, length us, event | category | flops | bytes accessed | tf_op | source)
XLA Modules:
  0.0 46.8 jit_solution(2318394696960412354)
XLA Ops:
  0.6 0.0 copy-start.6
  0.6 0.7 %pad.32 = f32[56]{0:T(128)S(1)} pad(f32[54]{0:T(128)} %param.16, f32[]{:T(128)} %constant.3.clone.1), padding=0_2 | pad | bytes 444 | tf_op jit(solution)/shard_map/jit(_pad)/pad | solution.py:290
  1.3 0.0 copy-done.6
  1.3 0.0 copy-start
  1.3 0.0 copy-start.2
  1.3 1.1 %multiply_reduce_fusion = f32[325]{0:T(512)S(1)} fusion(f32[53]{0:T(128)S(1)} %copy-done.6, s32[325,53]{0,1:T(8,128)} %param.13, s32[325,53]{0,1:T(8,128)} %param.12), kind=kLoop, calls=%fused_computation.4 | loop fusion | flops 68575 | bytes 139312 | tf_op jit(solution)/shard_map/reduce_sum | solution.py:286
  2.4 0.0 copy-start.4
  2.4 0.7 %copy-done.4 = f32[325]{0:T(512)S(1)} copy-done((f32[325]{0:T(512)S(1)}, f32[325]{0:T(512)}, u32[]{:S(2)}) %copy-start.4) | copy-done | bytes 1324
  3.1 0.0 copy-start.5
  3.1 0.7 %copy-done.5 = f32[325]{0:T(512)S(1)} copy-done((f32[325]{0:T(512)S(1)}, f32[325]{0:T(512)}, u32[]{:S(2)}) %copy-start.5) | copy-done | bytes 1324
  3.8 0.1 broadcast_in_dim.55.spread_ref
  3.9 0.0 copy-done
  3.9 0.0 copy-done.2
  3.9 0.0 copy-start.3
  3.9 0.8 %copy-done.3 = f32[54,2,128]{2,1,0:T(2,128)S(1)} copy-done((f32[54,2,128]{2,1,0:T(2,128)S(1)}, f32[54,2,128]{2,1,0:T(2,128)}, u32[]{:S(2)}) %copy-start.3) | copy-done | bytes 55320
  4.7 0.1 broadcast_in_dim.57
  4.8 0.1 reshape.61
  5.0 0.1 reshape.60
  5.1 0.1 broadcast_in_dim.56
  5.2 0.1 copy.29
  5.3 0.3 concatenate.12
  5.7 0.1 broadcast_in_dim.25
  5.8 0.0 copy-start.7
  5.8 0.1 broadcast_in_dim.26
  5.9 0.5 %copy-done.7 = s32[3]{0:T(128)S(1)} copy-done((s32[3]{0:T(128)S(1)}, s32[3]{0:T(128)}, u32[]{:S(2)}) %copy-start.7) | copy-done | bytes 36
  6.5 0.1 convert_convert_fusion
  6.6 0.0 copy-start.1
  6.6 1.0 %concatenate.13 = bf16[3,325,112]{2,1,0:T(8,128)(2,1)S(1)} concatenate(bf16[3,325,53]{2,1,0:T(8,128)(2,1)S(1)} %broadcast_in_dim.24, bf16[3,325,1]{2,1,0:T(8,128)(2,1)S(1)} %broadcast_in_dim.25, bf16[3,325,1]{2,1,0:T(8,128)(2,1)S(1)} %convert_convert_fusion, bf16[3,325,1]{2,1,0:T(8,128)(2,1)S(1)} %broadcast_in_dim.26, bf16[3,325,53]{2,1,0:T(8,128)(2,1)S(1)} %broadcast_in_dim.24, ...), dimensions={2} | concatenate | bytes 436800 | tf_op jit(solution)/shard_map/vmap()/concatenate | solution.py:278
  7.6 0.1 pad.30.w_tangent
  7.7 0.0 copy-done.1
  7.7 0.1 copy.41
  7.9 36.9 %step.1 = (f32[2,56,128]{2,1,0:T(8,128)S(1)}, f32[2,3,54,512]{3,2,1,0:T(8,128)S(1)}) custom-call(f32[2,56,128]{2,1,0:T(8,128)S(1)} %pad.27.s_ref, f32[2,3,56,512]{3,2,1,0:T(8,128)S(1)} %pad.28.t_ref, bf16[336,112]{1,0:T(8,128)(2,1)S(1)} %pad.29.w_nominal, bf16[3,336,112]{2,1,0:T(8,128)(2,1)S(1)} %pad.30.w_tangent, bf16[56,336]{1,0:T(8,128)(2,1)S(1)} %pad.31.w_net, ...), custom_call_target="tpu_custom_call" | custom-call | tf_op jit(solution)/shard_map/step/pallas_call | solution.py:294
  44.8 0.7 %copy.37 = f32[54,2,128]{2,1,0:T(2,128)} copy(f32[54,2,128]{2,0,1:T(8,128)S(1)} %slice_bitcast_fusion) | data formatting | bytes 110592
  45.5 1.4 %copy.38 = f32[3,54,2,512]{3,2,1,0:T(2,128)} copy(f32[3,54,2,512]{3,1,0,2:T(8,128)S(1)} %bitcast.11) | data formatting | bytes 1327104
  (15 shorter events, 0.2 us)
Async XLA Ops:
  0.6 0.7 %copy-start.6 = (f32[53]{0:T(128)S(1)}, f32[53]{0:T(128)}, u32[]{:S(2)}) copy-start(f32[53]{0:T(128)} %param.17) | copy-start | bytes 640
  1.3 2.5 %copy-start = (s32[325,53]{0,1:T(8,128)S(1)}, s32[325,53]{0,1:T(8,128)}, u32[]{:S(2)}) copy-start(s32[325,53]{0,1:T(8,128)} %param.12) | copy-start | bytes 206704
  1.3 2.5 %copy-start.2 = (s32[325,53]{0,1:T(8,128)S(1)}, s32[325,53]{0,1:T(8,128)}, u32[]{:S(2)}) copy-start(s32[325,53]{0,1:T(8,128)} %param.13) | copy-start | bytes 206704
  2.4 0.7 %copy-start.4 = (f32[325]{0:T(512)S(1)}, f32[325]{0:T(512)}, u32[]{:S(2)}) copy-start(f32[325]{0:T(512)} %param.14) | copy-start | bytes 3904
  3.1 0.7 %copy-start.5 = (f32[325]{0:T(512)S(1)}, f32[325]{0:T(512)}, u32[]{:S(2)}) copy-start(f32[325]{0:T(512)} %param.15) | copy-start | bytes 3904
  3.9 0.8 %copy-start.3 = (f32[54,2,128]{2,1,0:T(2,128)S(1)}, f32[54,2,128]{2,1,0:T(2,128)}, u32[]{:S(2)}) copy-start(f32[54,2,128]{2,1,0:T(2,128)} %param.9) | copy-start | bytes 165892
  5.8 0.7 %copy-start.7 = (s32[3]{0:T(128)S(1)}, s32[3]{0:T(128)}, u32[]{:S(2)}) copy-start(s32[3]{0:T(128)} %param.11) | copy-start | bytes 40
  6.6 1.1 %copy-start.1 = (f32[3,54,2,512]{3,2,1,0:T(2,128)S(1)}, f32[3,54,2,512]{3,2,1,0:T(2,128)}, u32[]{:S(2)}) copy-start(f32[3,54,2,512]{3,2,1,0:T(2,128)} %param.10) | copy-start | bytes 1990660

commit v2 on v1

v2 whole, which is shorter than its diff:
```python
import functools

import jax
import jax.numpy as jnp
from jax import lax
from jax.experimental import pallas as pl
from jax.experimental.pallas import tpu as pltpu
from jax.sharding import PartitionSpec as P

GRID_POINTS_THREE = 32
TIME_STEP = 0.2
ONE_LOW = 2.0**-10
MESH = pl.DeviceIdType.MESH
F32 = jnp.float32
BF16 = jnp.bfloat16


def in_plane(x, lane):
    cells = x.shape[1]
    width = GRID_POINTS_THREE
    before = jnp.where(
        lane == 0, pltpu.roll(x, cells - (width - 1), 1), pltpu.roll(x, 1, 1)
    )
    after = jnp.where(
        lane == width - 1, pltpu.roll(x, width - 1, 1), pltpu.roll(x, cells - 1, 1)
    )
    return before + after + (pltpu.roll(x, width, 1) + pltpu.roll(x, cells - width, 1))


def stacked(x, extra, species, row):
    base = species // 8 * 8
    tail = x[base:]
    tail = jnp.where(row == species + 1, 1.0 + ONE_LOW, jnp.where(row >= species, extra, tail))
    full = jnp.concatenate([x[:base], tail], 0)
    high = full.astype(BF16).astype(F32)
    return jnp.concatenate([high, full - high], 0).astype(BF16)


def halves(x):
    high = x.astype(BF16).astype(F32)
    return high, x - high


def with_heat(p, species, row):
    base = species // 8 * 8
    tail = p[base:]
    heat = p[species : species + 1] + p[species + 1 : species + 2]
    tail = jnp.where(row < species, tail, jnp.where(row == species, heat, 0.0))
    return jnp.concatenate([p[:base], tail], 0)


def column(vector, rows):
    count = vector.shape[0]
    wide = jnp.broadcast_to(vector.reshape(1, count), (rows, count))
    diagonal = lax.broadcasted_iota(jnp.int32, (rows, count), 0) == lax.broadcasted_iota(
        jnp.int32, (rows, count), 1
    )
    return jnp.sum(jnp.where(diagonal, wide, 0.0), axis=1, keepdims=True)


def build_weights(
    species, directions, react, product, lna, energy, diffus, enthalpy, index,
    w_nominal, w_tangent, w_net, spread, wide, flat,
):
    rows = w_net.shape[0]
    reactions = react.shape[1]
    depth = w_nominal.shape[0]
    nu_in = react[...].astype(F32)
    nu_net = (product[...] - react[...]).astype(F32)
    e_high, e_low = halves(energy[...].reshape(1, reactions))
    a_high, a_low = halves(lna[...].reshape(1, reactions))
    wide[...] = jnp.zeros_like(wide)
    for base, one in ((0, a_high), (rows, a_low * (1.0 / ONE_LOW))):
        wide[base : base + species, :reactions] = nu_in
        wide[base + species : base + species + 1, :reactions] = e_high
        wide[base + species + 1 : base + species + 2, :reactions] = one
        wide[base + species + 2 : base + species + 3, :reactions] = e_low
    nominal = jnp.transpose(wide[...])[:depth]
    w_nominal[...] = nominal.astype(BF16)
    reaction = lax.broadcasted_iota(jnp.int32, nominal.shape, 0)
    place = lax.broadcasted_iota(jnp.int32, nominal.shape, 1)
    cleared = jnp.where(
        (place == species + 1) | (place == rows + species + 1), 0.0, nominal
    )
    for d in range(directions):
        chosen = (reaction == index[d]) & (place == species + 1)
        w_tangent[d] = jnp.where(chosen, 1.0, cleared).astype(BF16)
    heat = -jnp.sum(nu_net * column(enthalpy[...], species), axis=0, keepdims=True)
    h_high, h_low = halves(heat)
    flat[...] = jnp.zeros_like(flat)
    flat[:species, :reactions] = nu_net
    flat[species : species + 1, :reactions] = h_high
    flat[species + 1 : species + 2, :reactions] = h_low
    w_net[...] = flat[...][:, :depth].astype(BF16)
    spread[...] = jnp.broadcast_to(column(diffus[...], rows), spread.shape)


def kernel(
    species, groups, ring,
    s_ref, t_ref, react_hbm, product_hbm, lna_hbm, energy_hbm, diffus_hbm, enthalpy_hbm, index,
    ns_ref, nt_ref,
    react, product, lna, energy, diffus, enthalpy,
    w_nominal, w_tangent, w_net, spread_ref, wide, flat,
    st, zs, mid, rates, prods, inverses, tt, mt, part, ns_full,
    st_send, st_recv, near_send, near_recv, far_send, far_recv, local_sem,
):
    directions = t_ref.shape[1]
    rows, cells = t_ref.shape[2], t_ref.shape[3]
    half = cells // 2
    own_cells = s_ref.shape[2]
    fields = species + 1
    base = species // 8 * 8
    g = lax.axis_index("grp")
    i = lax.axis_index("sp")
    odd = lax.rem(i, 2)
    partner = i + 1 - 2 * odd
    ahead = lax.rem(i + 2 - 4 * odd + ring, ring)
    behind = lax.rem(i - 2 + 4 * odd + ring, ring)
    near_side, far_side = 2 * (1 - odd), 2 * odd
    near_k, far_k = 3 * (1 - odd), 3 * odd
    peers = [lax.rem(g + k, groups) for k in range(1, groups)]

    def remote(src, dst, send, recv, target):
        return pltpu.make_async_remote_copy(
            src_ref=src, dst_ref=dst, send_sem=send, recv_sem=recv,
            device_id=target, device_id_type=MESH,
        )

    locals_ = [
        pltpu.make_async_copy(src, dst, local_sem.at[n])
        for n, (src, dst) in enumerate(
            [
                (t_ref, tt.at[pl.ds(2, 2)]), (s_ref, st.at[1, g]), (react_hbm, react),
                (product_hbm, product), (lna_hbm, lna), (energy_hbm, energy),
                (diffus_hbm, diffus), (enthalpy_hbm, enthalpy),
            ]
        )
    ]
    for copy in locals_[2:]:
        copy.start()

    barrier = pltpu.get_barrier_semaphore()
    for target in [(g, partner), (g, ahead), (g, behind)] + [(p, i) for p in peers]:
        pl.semaphore_signal(barrier, inc=1, device_id=target, device_id_type=MESH)
    for copy in locals_[:2]:
        copy.start()
    pl.semaphore_wait(barrier, 3 + len(peers))

    s_near = remote(s_ref, st.at[2 * odd, g], st_send.at[0], st_recv.at[2 * odd, g], (g, partner))
    s_near_in = remote(s_ref, st.at[near_side, g], st_send.at[0], st_recv.at[near_side, g], (g, partner))
    s_far = remote(st.at[near_side, g], st.at[far_side, g], st_send.at[1], st_recv.at[far_side, g], (g, ahead))

    def to_group(src, side, first):
        return [
            remote(src, st.at[side, g], st_send.at[first + k], st_recv.at[side, g], (p, i))
            for k, p in enumerate(peers)
        ]

    def piece(c):
        return c // 4, lax.rem(c // 2, 2), lax.rem(c, 2)

    def window(buffer, plane, d, h):
        return buffer.at[plane, d, :, pl.ds(pl.multiple_of(h * half, half), half)]

    def near(c):
        d, p, h = piece(c)
        return remote(
            window(t_ref, p, d, h), window(tt, 4 * odd + p, d, h),
            near_send.at[c], near_recv.at[c], (g, partner),
        )

    def far(c):
        d, p, h = piece(c)
        return remote(
            window(tt, 4 * (1 - odd) + p, d, h), window(tt, 4 * odd + p, d, h),
            far_send.at[c], far_recv.at[c], (g, ahead),
        )

    pieces = 4 * directions

    def forward(c):
        near(c).wait_recv()
        far(c).start()

    def span(low, high, step):
        lax.fori_loop(low, high, lambda c, carry: (step(c), carry)[1], 0)

    s_near.start()
    group_own = to_group(s_ref, 1, 2)
    for copy in group_own:
        copy.start()
    span(0, pieces, lambda c: near(c).start())

    for copy in locals_[2:]:
        copy.wait()
    build_weights(
        species, directions, react, product, lna, energy, diffus, enthalpy, index,
        w_nominal, w_tangent, w_net, spread_ref, wide, flat,
    )
    row = lax.broadcasted_iota(jnp.int32, (rows - base, cells), 0) + base
    lane = lax.rem(
        lax.broadcasted_iota(jnp.int32, (rows, cells), 1), jnp.int32(GRID_POINTS_THREE)
    )

    def arrived(side):
        for p in peers:
            remote(
                st.at[side, p], st.at[side, p], st_send.at[0], st_recv.at[side, p], (p, i)
            ).wait_recv()
        for q in range(groups):
            for p in range(2):
                zs[2 * side + p, :, q * own_cells : (q + 1) * own_cells] = st[side, q, p]

    def nominal(z, slot):
        level = 1.0 / z[species : species + 1]
        rate = jnp.exp(
            jnp.dot(
                w_nominal[...], stacked(z, -level, species, row), preferred_element_type=F32
            )
        )
        rates[slot] = rate
        high, low = halves(rate)
        production = jnp.dot(
            w_net[...], high.astype(BF16), preferred_element_type=F32
        ) + jnp.dot(w_net[...], low.astype(BF16), preferred_element_type=F32)
        inverse = jnp.exp(-z)
        inverse = jnp.concatenate([inverse[:base], jnp.where(row < species, inverse[base:], 1.0)], 0)
        inverses[slot] = inverse
        prods[slot] = jnp.concatenate(
            [production[:base], jnp.where(row < species, production[base:], 0.0)], 0
        )
        return with_heat(production, species, row) * inverse

    def tangent(u, z, slot, d):
        level = 1.0 / z[species : species + 1]
        change = jnp.dot(
            w_tangent[d],
            stacked(u, u[species : species + 1] * (level * level), species, row),
            preferred_element_type=F32,
        )
        moved = jnp.dot(
            w_net[...], (rates[slot] * change).astype(BF16), preferred_element_type=F32
        )
        return (with_heat(moved, species, row) - prods[slot] * u) * inverses[slot]

    def lap(low, x, high):
        return low + high + in_plane(x, lane) - 6.0 * x

    s_near_in.wait_recv()
    s_far.start()
    group_near = to_group(st.at[near_side, g], near_side, 2 + len(peers))
    for copy in group_near:
        copy.start()
    locals_[1].wait()
    arrived(1)
    for k in (1, 2):
        mid[k] = nominal(zs[k + 1], k)
    locals_[0].wait()
    span(0, 2, forward)
    s_far.wait_recv()
    group_far = to_group(st.at[far_side, g], far_side, 2 + 2 * len(peers))
    for copy in group_far:
        copy.start()
    span(2, 3, forward)

    def own_planes(d, carry):
        spread = spread_ref[...]
        for k in (1, 2):
            u = tt[k + 1, d]
            inner = tt[4 - k, d] + in_plane(u, lane) - 6.0 * u
            part[d, k - 1] = tangent(u, zs[k + 1], k, d) + spread * inner
        forward(3 + d)
        return carry

    lax.fori_loop(0, directions, own_planes, 0)
    done = 3 + directions

    arrived(near_side)
    mid[near_k] = nominal(zs[near_k + 1], near_k)
    span(done, done + 1, forward)
    arrived(far_side)
    mid[far_k] = nominal(zs[far_k + 1], far_k)
    for k in range(4):
        z = zs[k + 1]
        rate = mid[k] + spread_ref[...] * lap(zs[k], z, zs[k + 2])
        mid[k] = z + TIME_STEP * rate
        if k in (1, 2):
            ns_full[k - 1] = z + 0.5 * TIME_STEP * rate
    span(done + 1, done + 2, forward)
    for k in (1, 2):
        z = mid[k]
        rate = nominal(z, k + 3) + spread_ref[...] * lap(mid[k - 1], z, mid[k + 1])
        ns_full[k - 1] += 0.5 * TIME_STEP * rate
    for k in range(2):
        ns_ref[k] = ns_full[k, :, pl.ds(pl.multiple_of(g * own_cells, own_cells), own_cells)]
    span(done + 2, 4 * (directions - 1), forward)

    def halo(k, d):
        u = tt[k + 1, d]
        rate = tangent(u, zs[k + 1], k, d) + spread_ref[...] * lap(tt[k, d], u, tt[k + 2, d])
        mt[k] = u + TIME_STEP * rate

    def direction(d, carry):
        @pl.when(d == directions - 2)
        def _():
            span(4 * (directions - 1), pieces, forward)

        halo(near_k, d)
        span(4 * d, 4 * d + 4, lambda c: far(c).wait_recv())
        spread = spread_ref[...]
        halo(far_k, d)
        for k in (1, 2):
            u = tt[k + 1, d]
            rate = part[d, k - 1] + spread * tt[3 * k - 2, d]
            mt[k] = u + TIME_STEP * rate
            part[d, k - 1] = u + 0.5 * TIME_STEP * rate
        for k in (1, 2):
            u = mt[k]
            rate = tangent(u, mid[k], k + 3, d) + spread * lap(mt[k - 1], u, mt[k + 1])
            nt_ref[k - 1, d] = (part[d, k - 1] + 0.5 * TIME_STEP * rate)[:fields]
        return carry

    lax.fori_loop(0, directions, direction, 0)

    s_near.wait_send()
    s_far.wait_send()
    for copy in group_own + group_near + group_far:
        copy.wait_send()

    def sent(c):
        near(c).wait_send()
        far(c).wait_send()

    span(0, pieces, sent)


def shards(
    flame_state, tangents, direction_index, reactant_table, product_table,
    natural_log_frequency, arrhenius_energy, diffusivity, enthalpy,
):
    fields, planes, own_cells = flame_state.shape
    directions, cells = tangents.shape[0], tangents.shape[3]
    reactions, species = reactant_table.shape
    groups, ring = lax.axis_size("grp"), lax.axis_size("sp")
    assert planes == 2 and ring % 2 == 0 and directions >= 3
    rows = -(-(species + 3) // 8) * 8
    assert species % 8 <= 5
    depth = -(-reactions // 16) * 16
    lanes = -(-reactions // 128) * 128

    state = jnp.pad(flame_state.transpose(1, 0, 2), ((0, 0), (0, rows - fields), (0, 0)))
    sens = jnp.pad(tangents.transpose(2, 0, 1, 3), ((0, 0), (0, 0), (0, rows - fields), (0, 0)))

    vmem = pl.BlockSpec(memory_space=pltpu.VMEM)
    anywhere = pl.BlockSpec(memory_space=pl.ANY)
    hbm = pl.BlockSpec(memory_space=pltpu.HBM)
    smem = pl.BlockSpec(memory_space=pltpu.SMEM)
    pieces = 4 * directions
    new_state, new_sens = pl.pallas_call(
        functools.partial(kernel, species, groups, ring),
        out_shape=(
            jax.ShapeDtypeStruct((2, rows, own_cells), F32),
            jax.ShapeDtypeStruct((2, directions, fields, cells), F32),
        ),
        in_specs=[anywhere, anywhere] + [hbm] * 6 + [smem],
        out_specs=(vmem, vmem),
        scratch_shapes=[
            pltpu.VMEM((species, reactions), jnp.int32),
            pltpu.VMEM((species, reactions), jnp.int32),
            pltpu.VMEM((reactions,), F32),
            pltpu.VMEM((reactions,), F32),
            pltpu.VMEM((fields,), F32),
            pltpu.VMEM((species,), F32),
            pltpu.VMEM((depth, 2 * rows), BF16),
            pltpu.VMEM((directions, depth, 2 * rows), BF16),
            pltpu.VMEM((rows, depth), BF16),
            pltpu.VMEM((rows, cells), F32),
            pltpu.VMEM((2 * rows, lanes), F32),
            pltpu.VMEM((rows, lanes), F32),
            pltpu.VMEM((3, groups, 2, rows, own_cells), F32),
            pltpu.VMEM((6, rows, cells), F32),
            pltpu.VMEM((4, rows, cells), F32),
            pltpu.VMEM((6, depth, cells), F32),
            pltpu.VMEM((6, rows, cells), F32),
            pltpu.VMEM((6, rows, cells), F32),
            pltpu.VMEM((6, directions, rows, cells), F32),
            pltpu.VMEM((4, rows, cells), F32),
            pltpu.VMEM((directions, 2, rows, cells), F32),
            pltpu.VMEM((2, rows, cells), F32),
            pltpu.SemaphoreType.DMA((2 + 3 * (groups - 1),)),
            pltpu.SemaphoreType.DMA((3, groups)),
            pltpu.SemaphoreType.DMA((pieces,)),
            pltpu.SemaphoreType.DMA((pieces,)),
            pltpu.SemaphoreType.DMA((pieces,)),
            pltpu.SemaphoreType.DMA((pieces,)),
            pltpu.SemaphoreType.DMA((8,)),
        ],
        compiler_params=pltpu.CompilerParams(
            collective_id=0, has_side_effects=True, vmem_limit_bytes=48 << 20
        ),
        name="step",
    )(
        state, sens, reactant_table.T, product_table.T, natural_log_frequency,
        arrhenius_energy, diffusivity, enthalpy, direction_index,
    )
    return (
        new_state[:, :fields].transpose(1, 0, 2),
        new_sens.transpose(1, 2, 0, 3),
    )


def solution(mesh):
    in_specs = (
        P(None, "sp", "grp"), P("grp", None, "sp", None), P("grp"),
        P(), P(), P(), P(), P(), P(),
    )
    out_specs = (P(None, "sp", "grp"), P("grp", None, "sp", None))
    return jax.shard_map(shards, mesh=mesh, in_specs=in_specs, out_specs=out_specs, check_vma=False)
```

time: 47.1 us -> 36.5 us (0.77)
  Pallas kernels: 36.9 us -> 30.6 us
  local copies, waits for them, and re-layouts: 7.84 us -> 4.94 us
  other arithmetic: 1.25 us -> 0 us
    pallas_call x1, Pallas kernels: 36.9 us -> 30.6 us  [shards(): pl.pallas_call(functools.partial(kernel, species, groups, ring), out_shap...]
    concatenate x2 -> x0, local copies, waits for them, and re-layouts: 1.25 us -> none  [weights(): both = jnp.concatenate(half(one_high) + half(one_low), 1)]
    reduce_sum x1 -> x0, other arithmetic: 1.06 us -> none  [shards(): heat = -jnp.sum(nu_net * enthalpy[None, :], 1)]
    pad x4 -> x0, local copies, waits for them, and re-layouts: 0.75 us -> none  [the longest x1 0.66 us: shards(): jnp.pad(diffusivity, (0, rows - fields))[:, None]]
    broadcast_in_dim x7 -> x0, local copies, waits for them, and re-layouts: 0.55 us -> none  [the longest x4 0.27 us: weights(): both = jnp.concatenate(half(one_high) + half(one_low), 1)]
    unnamed x21 -> x18, local copies, waits for them, and re-layouts: 5.01 us -> 4.89 us
where the time goes in v2:
time: 36.5 us; the launch traced here: 36.3 us
  Pallas kernels  30.6 us (84%)
  local copies, waits for them, and re-layouts  4.94 us (14%)
  between operations  0.73 us (2%)
    pallas_call x1, Pallas kernels, shards(): pl.pallas_call(functools.partial(kernel, species, groups, ring), out_shap...  30.6 us
    unnamed x18, local copies, waits for them, and re-layouts  4.89 us

profile of v2, /device:TPU:0, one launch (start us, length us, event | category | flops | bytes accessed | tf_op | source)
XLA Modules:
  0.0 36.3 jit_solution(16014838892020812261)
XLA Ops:
  0.6 0.8 %copy.18 = f32[54,2,128]{2,0,1:T(8,128)S(1)} copy(f32[54,2,128]{2,1,0:T(2,128)} %param.9) | data formatting | bytes 110592 | tf_op args[0]
  1.5 1.2 %copy.17 = f32[3,54,2,512]{3,1,0,2:T(8,128)S(1)} copy(f32[3,54,2,512]{3,2,1,0:T(2,128)} %param.10) | data formatting | bytes 1327104 | tf_op args[1]
  2.7 0.0 copy-start
  2.7 0.0 copy-start.1
  2.7 0.0 copy-start.2
  2.7 0.0 copy-start.3
  2.7 0.0 copy-start.4
  2.7 0.0 copy-start.5
  2.8 0.0 copy-start.6
  2.8 0.8 %copy-done = s32[325,53]{0,1:T(8,128)S(1)} copy-done((s32[325,53]{0,1:T(8,128)S(1)}, s32[325,53]{0,1:T(8,128)}, u32[]{:S(2)}) %copy-start) | copy-done | bytes 68924
  3.6 0.0 copy-done.1
  3.6 0.0 copy-done.2
  3.6 0.0 copy-done.3
  3.6 0.0 copy-done.4
  3.6 0.0 copy-done.5
  3.6 0.0 copy-done.6
  3.6 30.6 %step.1 = (f32[2,56,128]{2,1,0:T(8,128)S(1)}, f32[2,3,54,512]{3,2,1,0:T(8,128)S(1)}) custom-call(f32[2,56,128]{2,1,0:T(8,128)S(1)} %pad.8.s_ref, f32[2,3,56,512]{3,2,1,0:T(8,128)S(1)} %pad.9.t_ref, s32[53,325]{1,0:T(8,128)S(1)} %bitcast.12, s32[53,325]{1,0:T(8,128)S(1)} %bitcast.13, f32[325]{0:T(512)S(1)} %copy-done.2, f32[325]{0:T(512)S(1)} %copy-done.3, ...), custom_call_target="tpu_custom_call" | custom-call | tf_op jit(solution)/shard_map/step/pallas_call | solution.py:359
  34.3 0.7 %copy.13 = f32[54,2,128]{2,1,0:T(2,128)} copy(f32[54,2,128]{2,0,1:T(8,128)S(1)} %slice_bitcast_fusion) | data formatting | bytes 110592
  34.9 1.4 %copy.14 = f32[3,54,2,512]{3,2,1,0:T(2,128)} copy(f32[3,54,2,512]{3,1,0,2:T(8,128)S(1)} %bitcast.11) | data formatting | bytes 1327104
  (3 shorter events, 0.1 us)
Async XLA Ops:
  2.7 0.9 %copy-start = (s32[325,53]{0,1:T(8,128)S(1)}, s32[325,53]{0,1:T(8,128)}, u32[]{:S(2)}) copy-start(s32[325,53]{0,1:T(8,128)} %param.12) | copy-start | bytes 206704
  2.7 0.9 %copy-start.1 = (s32[325,53]{0,1:T(8,128)S(1)}, s32[325,53]{0,1:T(8,128)}, u32[]{:S(2)}) copy-start(s32[325,53]{0,1:T(8,128)} %param.13) | copy-start | bytes 206704
  2.7 0.9 %copy-start.2 = (f32[325]{0:T(512)S(1)}, f32[325]{0:T(512)}, u32[]{:S(2)}) copy-start(f32[325]{0:T(512)} %lna_hbm.1) | copy-start | bytes 3904
  2.7 0.9 %copy-start.3 = (f32[325]{0:T(512)S(1)}, f32[325]{0:T(512)}, u32[]{:S(2)}) copy-start(f32[325]{0:T(512)} %energy_hbm.1) | copy-start | bytes 3904
  2.7 0.9 %copy-start.4 = (f32[54]{0:T(128)S(1)}, f32[54]{0:T(128)}, u32[]{:S(2)}) copy-start(f32[54]{0:T(128)} %diffus_hbm.1) | copy-start | bytes 652
  2.7 0.9 %copy-start.5 = (f32[53]{0:T(128)S(1)}, f32[53]{0:T(128)}, u32[]{:S(2)}) copy-start(f32[53]{0:T(128)} %enthalpy_hbm.1) | copy-start | bytes 640
  2.8 0.9 %copy-start.6 = (s32[3]{0:T(128)S(1)}, s32[3]{0:T(128)}, u32[]{:S(2)}) copy-start(s32[3]{0:T(128)} %index.1) | copy-start | bytes 40

commit v3 on v2

--- a/solution.py
+++ b/solution.py
@@ -1,4 +1,5 @@
 import functools
+import math
 
 import jax
 import jax.numpy as jnp
@@ -101,15 +102,15 @@
     ns_ref, nt_ref,
     react, product, lna, energy, diffus, enthalpy,
     w_nominal, w_tangent, w_net, spread_ref, wide, flat,
-    st, zs, mid, rates, prods, inverses, tt, mt, part, ns_full,
+    raw, st, zs, mid, rates, prods, inverses, tt, mt, part, ns_full,
     st_send, st_recv, near_send, near_recv, far_send, far_recv, local_sem,
 ):
-    directions = t_ref.shape[1]
-    rows, cells = t_ref.shape[2], t_ref.shape[3]
-    half = cells // 2
+    directions = t_ref.shape[0]
+    rows, cells = w_net.shape[0], zs.shape[2]
     own_cells = s_ref.shape[2]
     fields = species + 1
     base = species // 8 * 8
+    cuts = near_send.shape[0] // directions
     g = lax.axis_index("grp")
     i = lax.axis_index("sp")
     odd = lax.rem(i, 2)
@@ -130,7 +131,7 @@
         pltpu.make_async_copy(src, dst, local_sem.at[n])
         for n, (src, dst) in enumerate(
             [
-                (t_ref, tt.at[pl.ds(2, 2)]), (s_ref, st.at[1, g]), (react_hbm, react),
+                (t_ref, raw.at[1]), (s_ref, st.at[1, g]), (react_hbm, react),
                 (product_hbm, product), (lna_hbm, lna), (energy_hbm, energy),
                 (diffus_hbm, diffus), (enthalpy_hbm, enthalpy),
             ]
@@ -156,27 +157,30 @@
             for k, p in enumerate(peers)
         ]
 
-    def piece(c):
-        return c // 4, lax.rem(c // 2, 2), lax.rem(c, 2)
-
-    def window(buffer, plane, d, h):
-        return buffer.at[plane, d, :, pl.ds(pl.multiple_of(h * half, half), half)]
+    def window(buffer, c):
+        d, h = c // cuts, lax.rem(c, cuts)
+        return buffer.at[d, pl.ds(h * (fields // cuts), fields // cuts)]
 
     def near(c):
-        d, p, h = piece(c)
         return remote(
-            window(t_ref, p, d, h), window(tt, 4 * odd + p, d, h),
-            near_send.at[c], near_recv.at[c], (g, partner),
+            window(t_ref, c), window(raw.at[2 * odd], c), near_send.at[c], near_recv.at[c], (g, partner)
         )
 
     def far(c):
-        d, p, h = piece(c)
         return remote(
-            window(tt, 4 * (1 - odd) + p, d, h), window(tt, 4 * odd + p, d, h),
+            window(raw.at[near_side], c), window(raw.at[far_side], c),
             far_send.at[c], far_recv.at[c], (g, ahead),
         )
 
-    pieces = 4 * directions
+    def unpack(side, d):
+        block = raw[side, d]
+        block = jnp.concatenate([block, jnp.zeros((rows - fields,) + block.shape[1:], F32)], 0)
+        block = jnp.swapaxes(block, 0, 1)
+        for q in range(block.shape[0]):
+            lanes = block.shape[2]
+            tt[2 * side + q % 2, d, :, q // 2 * lanes : (q // 2 + 1) * lanes] = block[q]
+
+    pieces = cuts * directions
 
     def forward(c):
         near(c).wait_recv()
@@ -208,8 +212,11 @@
                 st.at[side, p], st.at[side, p], st_send.at[0], st_recv.at[side, p], (p, i)
             ).wait_recv()
         for q in range(groups):
+            slab = st[side, q]
+            slab = jnp.concatenate([slab, jnp.zeros((rows - fields,) + slab.shape[1:], F32)], 0)
+            slab = jnp.swapaxes(slab, 0, 1)
             for p in range(2):
-                zs[2 * side + p, :, q * own_cells : (q + 1) * own_cells] = st[side, q, p]
+                zs[2 * side + p, :, q * own_cells : (q + 1) * own_cells] = slab[p]
 
     def nominal(z, slot):
         level = 1.0 / z[species : species + 1]
@@ -256,24 +263,25 @@
     for k in (1, 2):
         mid[k] = nominal(zs[k + 1], k)
     locals_[0].wait()
-    span(0, 2, forward)
+    span(0, cuts // 2, forward)
     s_far.wait_recv()
     group_far = to_group(st.at[far_side, g], far_side, 2 + 2 * len(peers))
     for copy in group_far:
         copy.start()
-    span(2, 3, forward)
+    span(cuts // 2, cuts, forward)
 
     def own_planes(d, carry):
         spread = spread_ref[...]
+        unpack(1, d)
         for k in (1, 2):
             u = tt[k + 1, d]
             inner = tt[4 - k, d] + in_plane(u, lane) - 6.0 * u
             part[d, k - 1] = tangent(u, zs[k + 1], k, d) + spread * inner
-        forward(3 + d)
+        forward(cuts + d)
         return carry
 
     lax.fori_loop(0, directions, own_planes, 0)
-    done = 3 + directions
+    done = cuts + directions
 
     arrived(near_side)
     mid[near_k] = nominal(zs[near_k + 1], near_k)
@@ -291,9 +299,9 @@
         z = mid[k]
         rate = nominal(z, k + 3) + spread_ref[...] * lap(mid[k - 1], z, mid[k + 1])
         ns_full[k - 1] += 0.5 * TIME_STEP * rate
-    for k in range(2):
-        ns_ref[k] = ns_full[k, :, pl.ds(pl.multiple_of(g * own_cells, own_cells), own_cells)]
-    span(done + 2, 4 * (directions - 1), forward)
+    own = pl.ds(pl.multiple_of(g * own_cells, own_cells), own_cells)
+    ns_ref[...] = jnp.swapaxes(ns_full[:, :, own], 0, 1)[:fields]
+    span(done + 2, cuts * (directions - 1), forward)
 
     def halo(k, d):
         u = tt[k + 1, d]
@@ -303,10 +311,12 @@
     def direction(d, carry):
         @pl.when(d == directions - 2)
         def _():
-            span(4 * (directions - 1), pieces, forward)
-
+            span(cuts * (directions - 1), pieces, forward)
+
+        unpack(near_side, d)
         halo(near_k, d)
-        span(4 * d, 4 * d + 4, lambda c: far(c).wait_recv())
+        span(cuts * d, cuts * d + cuts, lambda c: far(c).wait_recv())
+        unpack(far_side, d)
         spread = spread_ref[...]
         halo(far_k, d)
         for k in (1, 2):
@@ -317,7 +327,12 @@
         for k in (1, 2):
             u = mt[k]
             rate = tangent(u, mid[k], k + 3, d) + spread * lap(mt[k - 1], u, mt[k + 1])
-            nt_ref[k - 1, d] = (part[d, k - 1] + 0.5 * TIME_STEP * rate)[:fields]
+            part[d, k - 1] += 0.5 * TIME_STEP * rate
+        lanes = t_ref.shape[3]
+        tiles = [
+            part[d, p, :, q * lanes : (q + 1) * lanes] for q in range(cells // lanes) for p in range(2)
+        ]
+        nt_ref[d] = jnp.swapaxes(jnp.stack(tiles, 0), 0, 1)[:fields]
         return carry
 
     lax.fori_loop(0, directions, direction, 0)
@@ -347,20 +362,21 @@
     assert species % 8 <= 5
     depth = -(-reactions // 16) * 16
     lanes = -(-reactions // 128) * 128
-
-    state = jnp.pad(flame_state.transpose(1, 0, 2), ((0, 0), (0, rows - fields), (0, 0)))
-    sens = jnp.pad(tangents.transpose(2, 0, 1, 3), ((0, 0), (0, 0), (0, rows - fields), (0, 0)))
+    tile = math.gcd(cells, 128)
+
+    sens = tangents.reshape(directions, fields, planes, cells // tile, tile).transpose(0, 1, 3, 2, 4)
+    sens = sens.reshape(directions, fields, planes * cells // tile, tile)
 
     vmem = pl.BlockSpec(memory_space=pltpu.VMEM)
     anywhere = pl.BlockSpec(memory_space=pl.ANY)
     hbm = pl.BlockSpec(memory_space=pltpu.HBM)
     smem = pl.BlockSpec(memory_space=pltpu.SMEM)
-    pieces = 4 * directions
+    pieces = math.gcd(fields, 6) * directions
     new_state, new_sens = pl.pallas_call(
         functools.partial(kernel, species, groups, ring),
         out_shape=(
-            jax.ShapeDtypeStruct((2, rows, own_cells), F32),
-            jax.ShapeDtypeStruct((2, directions, fields, cells), F32),
+            jax.ShapeDtypeStruct(flame_state.shape, F32),
+            jax.ShapeDtypeStruct(sens.shape, F32),
         ),
         in_specs=[anywhere, anywhere] + [hbm] * 6 + [smem],
         out_specs=(vmem, vmem),
@@ -377,7 +393,8 @@
             pltpu.VMEM((rows, cells), F32),
             pltpu.VMEM((2 * rows, lanes), F32),
             pltpu.VMEM((rows, lanes), F32),
-            pltpu.VMEM((3, groups, 2, rows, own_cells), F32),
+            pltpu.VMEM((3,) + sens.shape, F32),
+            pltpu.VMEM((3, groups) + flame_state.shape, F32),
             pltpu.VMEM((6, rows, cells), F32),
             pltpu.VMEM((4, rows, cells), F32),
             pltpu.VMEM((6, depth, cells), F32),
@@ -400,13 +417,11 @@
         ),
         name="step",
     )(
-        state, sens, reactant_table.T, product_table.T, natural_log_frequency,
+        flame_state, sens, reactant_table.T, product_table.T, natural_log_frequency,
         arrhenius_energy, diffusivity, enthalpy, direction_index,
     )
-    return (
-        new_state[:, :fields].transpose(1, 0, 2),
-        new_sens.transpose(1, 2, 0, 3),
-    )
+    new_sens = new_sens.reshape(directions, fields, cells // tile, planes, tile)
+    return new_state, new_sens.transpose(0, 1, 3, 2, 4).reshape(tangents.shape)
 
 
 def solution(mesh):

time: 36.5 us -> 37.5 us (1.027)
  local copies, waits for them, and re-layouts: 4.94 us -> 5.82 us
    unnamed x18 -> x20, local copies, waits for them, and re-layouts: 4.89 us -> 5.82 us
where the time goes in v3:
time: 37.5 us; the launch traced here: 37.2 us
  Pallas kernels  30.7 us (82%)
  local copies, waits for them, and re-layouts  5.82 us (16%)
  between operations  0.69 us (2%)
    pallas_call x1, Pallas kernels, shards(): pl.pallas_call(functools.partial(kernel, species, groups, ring), out_shap...  30.7 us
    unnamed x20, local copies, waits for them, and re-layouts  5.82 us

profile of v3, /device:TPU:0, one launch (start us, length us, event | category | flops | bytes accessed | tf_op | source)
XLA Modules:
  0.0 37.2 jit_solution(2338718315229404315)
XLA Ops:
  0.6 0.0 copy-start.5
  0.6 0.0 copy-start.4
  0.7 0.0 copy-start.6
  0.7 0.0 copy-start.7
  0.7 0.0 copy-start.8
  0.7 0.6 %copy-done.5 = f32[325]{0:T(512)S(1)} copy-done((f32[325]{0:T(512)S(1)}, f32[325]{0:T(512)}, u32[]{:S(2)}) %copy-start.5) | copy-done | bytes 1324
  1.3 0.0 copy-done.4
  1.3 0.0 copy-done.6
  1.3 0.0 copy-done.7
  1.3 0.0 copy-done.8
  1.4 0.0 copy-start
  1.4 1.1 %copy-done = f32[3,54,2,512]{3,2,1,0:T(2,128)S(1)} copy-done((f32[3,54,2,512]{3,2,1,0:T(2,128)S(1)}, f32[3,54,2,512]{3,2,1,0:T(2,128)}, u32[]{:S(2)}) %copy-start) | copy-done | bytes 663576
  2.4 0.0 copy-start.1
  2.4 0.9 %copy-done.1 = s32[325,53]{0,1:T(8,128)S(1)} copy-done((s32[325,53]{0,1:T(8,128)S(1)}, s32[325,53]{0,1:T(8,128)}, u32[]{:S(2)}) %copy-start.1) | copy-done | bytes 68924
  3.3 0.0 copy-start.2
  3.3 0.9 %copy-done.2 = s32[325,53]{0,1:T(8,128)S(1)} copy-done((s32[325,53]{0,1:T(8,128)S(1)}, s32[325,53]{0,1:T(8,128)}, u32[]{:S(2)}) %copy-start.2) | copy-done | bytes 68924
  4.2 0.0 copy-start.3
  4.2 0.8 %copy-done.3 = f32[54,2,128]{2,1,0:T(2,128)S(1)} copy-done((f32[54,2,128]{2,1,0:T(2,128)S(1)}, f32[54,2,128]{2,1,0:T(2,128)}, u32[]{:S(2)}) %copy-start.3) | copy-done | bytes 55320
  5.0 30.7 %step.1 = (f32[54,2,128]{2,1,0:T(2,128)S(1)}, f32[3,54,8,128]{3,2,1,0:T(8,128)S(1)}) custom-call(f32[54,2,128]{2,1,0:T(2,128)S(1)} %copy-done.3, f32[3,54,8,128]{3,2,1,0:T(8,128)S(1)} %bitcast.13, s32[53,325]{1,0:T(8,128)S(1)} %bitcast.14, s32[53,325]{1,0:T(8,128)S(1)} %bitcast.15, f32[325]{0:T(512)S(1)} %copy-done.4, f32[325]{0:T(512)S(1)} %copy-done.5, ...), custom_call_target="tpu_custom_call" | custom-call | tf_op jit(solution)/shard_map/step/pallas_call | solution.py:375
  35.7 0.6 %copy.15 = f32[54,2,128]{2,1,0:T(2,128)} copy(f32[54,2,128]{2,1,0:T(2,128)S(1)} %get-tuple-element.8) | data formatting | bytes 110592
  36.3 0.8 %copy.16 = f32[3,54,2,512]{3,2,1,0:T(2,128)} copy(f32[3,54,2,512]{3,2,1,0:T(2,128)S(1)} %bitcast.12) | data formatting | bytes 1327104
Async XLA Ops:
  0.6 0.7 %copy-start.5 = (f32[325]{0:T(512)S(1)}, f32[325]{0:T(512)}, u32[]{:S(2)}) copy-start(f32[325]{0:T(512)} %energy_hbm.1) | copy-start | bytes 3904
  0.6 0.7 %copy-start.4 = (f32[325]{0:T(512)S(1)}, f32[325]{0:T(512)}, u32[]{:S(2)}) copy-start(f32[325]{0:T(512)} %lna_hbm.1) | copy-start | bytes 3904
  0.7 0.7 %copy-start.6 = (f32[54]{0:T(128)S(1)}, f32[54]{0:T(128)}, u32[]{:S(2)}) copy-start(f32[54]{0:T(128)} %diffus_hbm.1) | copy-start | bytes 652
  0.7 0.7 %copy-start.7 = (f32[53]{0:T(128)S(1)}, f32[53]{0:T(128)}, u32[]{:S(2)}) copy-start(f32[53]{0:T(128)} %enthalpy_hbm.1) | copy-start | bytes 640
  0.7 0.7 %copy-start.8 = (s32[3]{0:T(128)S(1)}, s32[3]{0:T(128)}, u32[]{:S(2)}) copy-start(s32[3]{0:T(128)} %index.1) | copy-start | bytes 40
  1.4 1.1 %copy-start = (f32[3,54,2,512]{3,2,1,0:T(2,128)S(1)}, f32[3,54,2,512]{3,2,1,0:T(2,128)}, u32[]{:S(2)}) copy-start(f32[3,54,2,512]{3,2,1,0:T(2,128)} %param.10) | copy-start | bytes 1990660
  2.4 0.9 %copy-start.1 = (s32[325,53]{0,1:T(8,128)S(1)}, s32[325,53]{0,1:T(8,128)}, u32[]{:S(2)}) copy-start(s32[325,53]{0,1:T(8,128)} %param.12) | copy-start | bytes 206704
  3.3 0.9 %copy-start.2 = (s32[325,53]{0,1:T(8,128)S(1)}, s32[325,53]{0,1:T(8,128)}, u32[]{:S(2)}) copy-start(s32[325,53]{0,1:T(8,128)} %param.13) | copy-start | bytes 206704
  4.2 0.8 %copy-start.3 = (f32[54,2,128]{2,1,0:T(2,128)S(1)}, f32[54,2,128]{2,1,0:T(2,128)}, u32[]{:S(2)}) copy-start(f32[54,2,128]{2,1,0:T(2,128)} %s_ref.1) | copy-start | bytes 165892

commit v4 on v3

--- a/solution.py
+++ b/solution.py
@@ -413,7 +413,8 @@
             pltpu.SemaphoreType.DMA((8,)),
         ],
         compiler_params=pltpu.CompilerParams(
-            collective_id=0, has_side_effects=True, vmem_limit_bytes=48 << 20
+            collective_id=0, has_side_effects=True, vmem_limit_bytes=67043328
+
         ),
         name="step",
     )(

time: 37.5 us -> 36.2 us (0.965)
  local copies, waits for them, and re-layouts: 5.82 us -> 3.6 us
  Pallas kernels: 30.7 us -> 31.7 us
    unnamed x20 -> x2, local copies, waits for them, and re-layouts: 5.82 us -> 3.6 us
    pallas_call x1, Pallas kernels: 30.7 us -> 31.7 us  [shards(): pl.pallas_call(functools.partial(kernel, species, groups, ring), out_shap...]
where the time goes in v4:
time: 36.2 us; the launch traced here: 36 us
  Pallas kernels  31.7 us (88%)
  local copies, waits for them, and re-layouts  3.6 us (10%)
  between operations  0.64 us (2%)
    pallas_call x1, Pallas kernels, shards(): pl.pallas_call(functools.partial(kernel, species, groups, ring), out_shap...  31.7 us
    unnamed x2, local copies, waits for them, and re-layouts  3.6 us

profile of v4, /device:TPU:0, one launch (start us, length us, event | category | flops | bytes accessed | tf_op | source)
XLA Modules:
  0.0 36.0 jit_solution(4666804259809848080)
XLA Ops:
  0.6 31.7 %step.1 = (f32[54,2,128]{2,1,0:T(2,128)}, f32[3,54,8,128]{3,2,1,0:T(8,128)}) custom-call(f32[54,2,128]{2,1,0:T(2,128)} %s_ref.1, f32[3,54,8,128]{3,2,1,0:T(8,128)} %bitcast.13, s32[53,325]{1,0:T(8,128)} %bitcast.14, s32[53,325]{1,0:T(8,128)} %bitcast.15, f32[325]{0:T(512)} %lna_hbm.1, f32[325]{0:T(512)} %energy_hbm.1, f32[54]{0:T(128)} %diffus_hbm.1, ...), custom_call_target="tpu_custom_call" | custom-call | tf_op jit(solution)/shard_map/step/pallas_call | solution.py:375
  32.4 1.4 %copy.15 = f32[54,2,128]{2,1,0:T(2,128)} copy(f32[54,2,128]{2,1,0:T(2,128)} %get-tuple-element.8) | data formatting | bytes 110592
  33.8 2.2 %copy.16 = f32[3,54,2,512]{3,2,1,0:T(2,128)} copy(f32[3,54,2,512]{3,2,1,0:T(2,128)} %bitcast.12) | data formatting | bytes 1327104

commit v5 on v3

--- a/solution.py
+++ b/solution.py
@@ -98,8 +98,8 @@
 
 def kernel(
     species, groups, ring,
-    s_ref, t_ref, react_hbm, product_hbm, lna_hbm, energy_hbm, diffus_hbm, enthalpy_hbm, index,
-    ns_ref, nt_ref,
+    s_ref, t_ref, react_hbm, product_hbm, lna_hbm, energy_hbm, diffus_hbm, enthalpy_hbm, index_hbm,
+    ns_ref, nt_ref, index,
     react, product, lna, energy, diffus, enthalpy,
     w_nominal, w_tangent, w_net, spread_ref, wide, flat,
     raw, st, zs, mid, rates, prods, inverses, tt, mt, part, ns_full,
@@ -134,6 +134,7 @@
                 (t_ref, raw.at[1]), (s_ref, st.at[1, g]), (react_hbm, react),
                 (product_hbm, product), (lna_hbm, lna), (energy_hbm, energy),
                 (diffus_hbm, diffus), (enthalpy_hbm, enthalpy),
+                (index_hbm, index),
             ]
         )
     ]
@@ -370,7 +371,6 @@
     vmem = pl.BlockSpec(memory_space=pltpu.VMEM)
     anywhere = pl.BlockSpec(memory_space=pl.ANY)
     hbm = pl.BlockSpec(memory_space=pltpu.HBM)
-    smem = pl.BlockSpec(memory_space=pltpu.SMEM)
     pieces = math.gcd(fields, 6) * directions
     new_state, new_sens = pl.pallas_call(
         functools.partial(kernel, species, groups, ring),
@@ -378,9 +378,10 @@
             jax.ShapeDtypeStruct(flame_state.shape, F32),
             jax.ShapeDtypeStruct(sens.shape, F32),
         ),
-        in_specs=[anywhere, anywhere] + [hbm] * 6 + [smem],
+        in_specs=[anywhere, anywhere] + [hbm] * 7,
         out_specs=(vmem, vmem),
         scratch_shapes=[
+            pltpu.SMEM((directions,), jnp.int32),
             pltpu.VMEM((species, reactions), jnp.int32),
             pltpu.VMEM((species, reactions), jnp.int32),
             pltpu.VMEM((reactions,), F32),
@@ -410,15 +411,20 @@
             pltpu.SemaphoreType.DMA((pieces,)),
             pltpu.SemaphoreType.DMA((pieces,)),
             pltpu.SemaphoreType.DMA((pieces,)),
-            pltpu.SemaphoreType.DMA((8,)),
+            pltpu.SemaphoreType.DMA((9,)),
         ],
         compiler_params=pltpu.CompilerParams(
             collective_id=0, has_side_effects=True, vmem_limit_bytes=48 << 20
         ),
         name="step",
     )(
-        flame_state, sens, reactant_table.T, product_table.T, natural_log_frequency,
-        arrhenius_energy, diffusivity, enthalpy, direction_index,
+        *[
+            pltpu.with_memory_space_constraint(x, pltpu.HBM)
+            for x in (
+                flame_state, sens, reactant_table.T, product_table.T, natural_log_frequency,
+                arrhenius_energy, diffusivity, enthalpy, direction_index,
+            )
+        ],
     )
     new_sens = new_sens.reshape(directions, fields, cells // tile, planes, tile)
     return new_state, new_sens.transpose(0, 1, 3, 2, 4).reshape(tangents.shape)

time: 37.5 us -> 32.4 us (0.86)
  local copies, waits for them, and re-layouts: 5.82 us -> 1.46 us
  Pallas kernels: 30.7 us -> 30.2 us
    unnamed x20 -> x2, local copies, waits for them, and re-layouts: 5.82 us -> 1.46 us
    pallas_call x1, Pallas kernels: 30.7 us -> 30.2 us  [shards(): pl.pallas_call(functools.partial(kernel, species, groups, ring), out_shap...]
where the time goes in v5:
time: 32.4 us; the launch traced here: 32.3 us
  Pallas kernels  30.2 us (93%)
  local copies, waits for them, and re-layouts  1.46 us (5%)
  between operations  0.64 us (2%)
    pallas_call x1, Pallas kernels, shards(): pl.pallas_call(functools.partial(kernel, species, groups, ring), out_shap...  30.2 us
    unnamed x2, local copies, waits for them, and re-layouts  1.46 us

profile of v5, /device:TPU:0, one launch (start us, length us, event | category | flops | bytes accessed | tf_op | source)
XLA Modules:
  0.0 32.3 jit_solution(2792587256501163746)
XLA Ops:
  0.6 30.2 %step.1 = (f32[54,2,128]{2,1,0:T(2,128)S(1)}, f32[3,54,8,128]{3,2,1,0:T(8,128)S(1)}) custom-call(f32[54,2,128]{2,1,0:T(2,128)} %s_ref.1, f32[3,54,8,128]{3,2,1,0:T(8,128)} %bitcast.13, s32[53,325]{1,0:T(8,128)} %bitcast.14, s32[53,325]{1,0:T(8,128)} %bitcast.15, f32[325]{0:T(512)} %lna_hbm.1, f32[325]{0:T(512)} %energy_hbm.1, f32[54]{0:T(128)} %diffus_hbm.1, ...), custom_call_target="tpu_custom_call" | custom-call | tf_op jit(solution)/shard_map/step/pallas_call | solution.py:375
  30.8 0.6 %copy.15 = f32[54,2,128]{2,1,0:T(2,128)} copy(f32[54,2,128]{2,1,0:T(2,128)S(1)} %get-tuple-element.8) | data formatting | bytes 110592
  31.4 0.8 %copy.16 = f32[3,54,2,512]{3,2,1,0:T(2,128)} copy(f32[3,54,2,512]{3,2,1,0:T(2,128)S(1)} %bitcast.12) | data formatting | bytes 1327104

commit v6 on v5

--- a/solution.py
+++ b/solution.py
@@ -371,7 +371,7 @@
     vmem = pl.BlockSpec(memory_space=pltpu.VMEM)
     anywhere = pl.BlockSpec(memory_space=pl.ANY)
     hbm = pl.BlockSpec(memory_space=pltpu.HBM)
-    pieces = math.gcd(fields, 6) * directions
+    pieces = math.gcd(fields, 9) * directions
     new_state, new_sens = pl.pallas_call(
         functools.partial(kernel, species, groups, ring),
         out_shape=(

time: 32.4 us -> 33.3 us (1.028)
  Pallas kernels: 30.2 us -> 31 us
    pallas_call x1, Pallas kernels: 30.2 us -> 31 us  [shards(): pl.pallas_call(functools.partial(kernel, species, groups, ring), out_shap...]
where the time goes in v6:
time: 33.3 us; the launch traced here: 33.1 us
  Pallas kernels  31 us (93%)
  local copies, waits for them, and re-layouts  1.46 us (4%)
  between operations  0.64 us (2%)
    pallas_call x1, Pallas kernels, shards(): pl.pallas_call(functools.partial(kernel, species, groups, ring), out_shap...  31 us
    unnamed x2, local copies, waits for them, and re-layouts  1.46 us

profile of v6, /device:TPU:0, one launch (start us, length us, event | category | flops | bytes accessed | tf_op | source)
XLA Modules:
  0.0 33.1 jit_solution(2856855068197270053)
XLA Ops:
  0.6 31.0 %step.1 = (f32[54,2,128]{2,1,0:T(2,128)S(1)}, f32[3,54,8,128]{3,2,1,0:T(8,128)S(1)}) custom-call(f32[54,2,128]{2,1,0:T(2,128)} %s_ref.1, f32[3,54,8,128]{3,2,1,0:T(8,128)} %bitcast.13, s32[53,325]{1,0:T(8,128)} %bitcast.14, s32[53,325]{1,0:T(8,128)} %bitcast.15, f32[325]{0:T(512)} %lna_hbm.1, f32[325]{0:T(512)} %energy_hbm.1, f32[54]{0:T(128)} %diffus_hbm.1, ...), custom_call_target="tpu_custom_call" | custom-call | tf_op jit(solution)/shard_map/step/pallas_call | solution.py:375
  31.7 0.6 %copy.15 = f32[54,2,128]{2,1,0:T(2,128)} copy(f32[54,2,128]{2,1,0:T(2,128)S(1)} %get-tuple-element.8) | data formatting | bytes 110592
  32.3 0.8 %copy.16 = f32[3,54,2,512]{3,2,1,0:T(2,128)} copy(f32[3,54,2,512]{3,2,1,0:T(2,128)S(1)} %bitcast.12) | data formatting | bytes 1327104
